TPU v7x, 256 devices: a whole 4x4x8 slice. The times are simulated.
256 devices in a mesh: gx: 128 (over x, z, y), gy: 2 (over core).
Axes of the slice: x: 4, y: 4, z: 8, core: 2. Of those that a mesh axis runs over, the one named last changes fastest.
Arguments:
- records: float32 [786432, 128], P('gx', 'gy'), may hold values from -1.8 to 1.8
- idents: float32 [524288, 128], P('gx', 'gy'), may hold values from -1.8 to 1.8
- rec_count: int32 [786432], P('gx'), may hold values from 1 to 1000
- id_count: int32 [524288], P('gx'), may hold values from 1 to 1000
- observed: bfloat16 [24576, 128, 128], P('gx'), may hold values from -6 to 6
- send_list: int32 [16384, 1], P('gx'), may hold values from 0 to 47
- slot_of_block: int32 [24576], P('gx'), may hold values from 0 to 127, as said below
- id_of_block: int32 [24576], P('gx'), may hold values from 0 to 31
Outputs:
- new_records: float32 [786432, 128], P('gx', 'gy')
- new_idents: float32 [524288, 128], P('gx', 'gy')
Inputs may be any that keep to these rules, and one draw needn't show every extreme that they name: `slot_of_block`: each owner's 192 entries use every slot from 0 to 127.
All inputs are finite; a program needn't handle non-finite values.
Results may differ from a plain program's by a relative error of at most 0.013.
Values may be sent and summed in bfloat16 or wider, within the bound.
No kernel may reach another device: no remote copies, remote signals or barrier semaphores. Data moves between devices by JAX's collectives and lax.ppermute only.
A program may use at most 128 MiB of HBM per device.

v0:
```python
import jax
import jax.numpy as jnp
from jax import lax
from jax.sharding import PartitionSpec as P


def residual_of(summed, row_weight, col_weight, block_obs):
    weight_grid = row_weight[:, :, None] * col_weight[:, None, :]
    return (weight_grid * (summed - block_obs.astype(jnp.float32))).astype(jnp.bfloat16)


def body(records, idents, rec_count, id_count, observed, send_list, slot_of_block, id_of_block):
    peers = lax.axis_size("gx")
    blk_rows = observed.shape[1]
    half_cols = records.shape[1]
    slot_count = send_list.shape[1]
    received = peers * slot_count
    log_top = jnp.log(jnp.float32(1001.0))
    rec_bf = records.astype(jnp.bfloat16).reshape(-1, blk_rows, half_cols)
    id_bf = idents.astype(jnp.bfloat16).reshape(-1, blk_rows, half_cols)
    rec_weight = (
        (jnp.log1p(rec_count.astype(jnp.float32)) / log_top)
        .astype(jnp.bfloat16)
        .reshape(-1, blk_rows)
    )
    id_weight = (jnp.log1p(id_count.astype(jnp.float32)) / log_top).reshape(-1, blk_rows)
    sent_rows = rec_bf[send_list].reshape(peers, slot_count, blk_rows * half_cols)
    sent_weight = rec_weight[send_list]
    arrived, arrived_weight = (
        lax.all_to_all(sent_rows, "gx", split_axis=0, concat_axis=0, tiled=True),
        lax.all_to_all(sent_weight, "gx", split_axis=0, concat_axis=0, tiled=True),
    )
    left_all = arrived.reshape(received, blk_rows, half_cols)
    weight_all = arrived_weight.reshape(received, blk_rows).astype(jnp.float32)
    left_rows = left_all[slot_of_block]
    right_rows = id_bf[id_of_block]
    partial_value = jnp.einsum(
        "bik,bjk->bij", left_rows, right_rows, preferred_element_type=jnp.float32
    ).astype(jnp.bfloat16)
    summed = lax.psum(partial_value, "gy").astype(jnp.float32)
    resid = residual_of(summed, weight_all[slot_of_block], id_weight[id_of_block], observed)
    grad_left = jnp.einsum("bij,bjk->bik", resid, right_rows, preferred_element_type=jnp.float32)
    grad_right = jnp.einsum("bij,bik->bjk", resid, left_rows, preferred_element_type=jnp.float32)
    slot_grad = (
        jnp.zeros((received, blk_rows, half_cols), jnp.float32).at[slot_of_block].add(grad_left)
    )
    id_grad = jnp.zeros(id_bf.shape, jnp.float32).at[id_of_block].add(grad_right)
    returned = lax.all_to_all(
        slot_grad.reshape(peers, slot_count, blk_rows * half_cols).astype(jnp.bfloat16),
        "gx",
        split_axis=0,
        concat_axis=0,
        tiled=True,
    ).astype(jnp.float32)
    rec_grad = jnp.zeros((rec_bf.shape[0], blk_rows * half_cols), jnp.float32)
    rec_grad = rec_grad.at[send_list.reshape(-1)].add(
        returned.reshape(received, blk_rows * half_cols)
    )
    new_records = records - 0.05 * (rec_grad.reshape(records.shape) + 0.1 * records)
    new_idents = idents - 0.05 * (id_grad.reshape(idents.shape) + 0.1 * idents)
    return (new_records, new_idents)


def solution(mesh):
    in_specs = (
        P("gx", "gy"),
        P("gx", "gy"),
        P("gx"),
        P("gx"),
        P("gx", None, None),
        P("gx", None),
        P("gx"),
        P("gx"),
    )
    out_specs = (P("gx", "gy"), P("gx", "gy"))
    return jax.shard_map(body, mesh=mesh, in_specs=in_specs, out_specs=out_specs, check_vma=False)
```

profile of v0, /device:TPU:1, one launch (start us, length us, event | category | flops | bytes accessed | tf_op | source)
XLA Modules:
  0.0 344.2 jit_solution(12492377144656570057)
XLA Ops:
  7.2 0.7 fusion.9
  7.8 1.6 copy_bitcast_fusion
  9.4 1.0 gather_fusion.3
  10.4 3.4 copy.30
  13.8 0.5 broadcast.42
  14.3 3.9 %reduce = bf16[128,8192]{0,1:T(8,128)(2,1)S(1)} reduce(bf16[128,1,8192]{0,2,1:T(8,128)(2,1)} %bitcast.40, bf16[]{:T(256)} %broadcast.42), dimensions={1}, to_apply=%copy.31.reduce_sub_computation | reduce | bytes 4194306 | tf_op jit(solution)/shard_map/reshape | solution.py:27
  18.2 2.9 copy.53
  21.2 4.5 %reshape.150 = bf16[128,2,4096]{2,1,0:T(2,128)(2,1)} reshape(bf16[128,8192]{1,0:T(8,128)(2,1)} %copy.53) | data formatting | bytes 4194304
  25.7 16.3 %all-to-all-start.1 = ((bf16[128,2,4096]{2,1,0:T(2,128)(2,1)}), bf16[128,2,4096]{2,1,0:T(2,128)(2,1)S(1)}, u32[]{:S(2)}, u32[]{:S(2)}) async-start(bf16[128,2,4096]{2,1,0:T(2,128)(2,1)} %reshape.150), calls=%async_computation.1 | async-start | bytes 4194304 | tf_op jit(solution)/shard_map/all_to_all | solution.py:30
  42.0 0.0 all-reduce.2.cloned.1.call-start
  42.1 1.3 copy_bitcast_fusion.1
  43.4 2.7 gather_fusion.5
  46.2 45.1 %all-to-all-done.1 = bf16[128,2,4096]{2,1,0:T(2,128)(2,1)S(1)} async-done(((bf16[128,2,4096]{2,1,0:T(2,128)(2,1)}), bf16[128,2,4096]{2,1,0:T(2,128)(2,1)S(1)}, u32[]{:S(2)}, u32[]{:S(2)}) %all-to-all-start.1) | async-done | bytes 2097184 | tf_op jit(solution)/shard_map/all_to_all | solution.py:30
  91.3 6.8 %reshape.151 = bf16[128,1,8192]{2,1,0:T(2,128)(2,1)} reshape(bf16[128,2,4096]{2,1,0:T(2,128)(2,1)S(1)} %all-to-all-done.1) | data formatting | bytes 4194304
  98.0 8.8 %copy.32 = bf16[128,1,8192]{0,2,1:T(8,128)(2,1)S(1)} copy(bf16[128,1,8192]{2,1,0:T(2,128)(2,1)} %reshape.151) | data formatting | bytes 4194304 | tf_op jit(solution)/shard_map/all_to_all | solution.py:30
  106.8 3.4 copy.33
  110.2 2.7 gather_fusion.4
  113.0 6.4 %convolution_convert_fusion = bf16[192,128,128]{2,1,0:T(8,128)(2,1)} fusion(bf16[192,128,64]{1,2,0:T(8,128)(2,1)S(1)} %gather_fusion.4, bf16[192,128,64]{1,2,0:T(8,128)(2,1)} %gather_fusion.5), kind=kOutput, calls=%fused_computation.13 | convolution fusion | flops 405798912 | bytes 12582912 | tf_op jit(solution)/shard_map/bik,bjk->bij/dot_general | solution.py:37
  119.4 0.0 all-reduce.2.cloned.1.call-update
  119.5 0.7 copy-done.2
  120.2 0.7 gather_fusion
  120.9 0.7 copy.27
  121.6 10.0 %all-to-all-start = ((bf16[128,1,128]{2,1,0:T(2,128)(2,1)}), bf16[128,1,128]{2,1,0:T(2,128)(2,1)S(1)}, u32[]{:S(2)}, u32[]{:S(2)}) async-start(bf16[128,1,128]{2,1,0:T(2,128)(2,1)} %copy.27), calls=%async_computation | async-start | bytes 131072 | tf_op jit(solution)/shard_map/all_to_all | solution.py:31
  131.6 0.7 gather_fusion.2
  132.3 9.6 %all-to-all-done = bf16[128,1,128]{2,1,0:T(2,128)(2,1)S(1)} async-done(((bf16[128,1,128]{2,1,0:T(2,128)(2,1)}), bf16[128,1,128]{2,1,0:T(2,128)(2,1)S(1)}, u32[]{:S(2)}, u32[]{:S(2)}) %all-to-all-start) | async-done | bytes 32800 | tf_op jit(solution)/shard_map/all_to_all | solution.py:31
  141.9 0.7 gather_fusion.1
  142.6 18.4 %all-reduce.2.cloned.1.call-done = bf16[192,128,128]{2,1,0:T(8,128)(2,1)} async-done(((bf16[192,128,128]{2,1,0:T(8,128)(2,1)}), bf16[192,128,128]{2,1,0:T(8,128)(2,1)}) %all-reduce.2.cloned.1.call-update) | async-done | bytes 6291472 | tf_op jit(solution)/shard_map/psum | solution.py:40
  161.0 11.0 %fusion.6 = f32[192,128,64]{1,2,0:T(8,128)} fusion(bf16[192,128,64]{1,2,0:T(8,128)(2,1)} %gather_fusion.5, bf16[192,128,128]{2,1,0:T(8,128)(2,1)} %param.12, bf16[192,128,128]{2,1,0:T(8,128)(2,1)} %all-reduce.2.cloned.1.call-done, f32[192,128]{1,0:T(8,128)S(1)} %gather_fusion.2, f32[192,128]{1,0:T(8,128)S(1)} %gather_fusion.1), kind=kOutput, calls=%fused_computation.19 | convolution fusion | flops 421527552 | bytes 22216704 | tf_op jit(solution)/shard_map/bij,bjk->bik/dot_general | solution.py:42
  172.0 2.5 broadcast_in_dim.13
  174.5 29.9 %scatter_fusion = f32[128,128,64]{1,2,0:T(8,128)} fusion(f32[128,128,64]{1,2,0:T(8,128)} %broadcast_in_dim.13, s32[192]{0:T(256)S(1)} %compare_select_fusion.1, f32[192,128,64]{1,2,0:T(8,128)} %fusion.6), kind=kCustom, calls=%fused_computation.6 | custom fusion | flops 1572864 | bytes 18875136 | tf_op jit(solution)/shard_map/scatter-add | solution.py:45
  204.5 4.0 %convert_element_type.59 = bf16[128,128,64]{1,2,0:T(8,128)(2,1)} convert(f32[128,128,64]{1,2,0:T(8,128)} %scatter_fusion) | non-fusion elementwise | flops 1048576 | bytes 6291456 | tf_op jit(solution)/shard_map/convert_element_type | solution.py:49
  208.5 4.6 %copy.35 = bf16[128,128,64]{0,2,1:T(8,128)(2,1)} copy(bf16[128,128,64]{1,2,0:T(8,128)(2,1)} %convert_element_type.59) | data formatting | bytes 4194304 | tf_op jit(solution)/shard_map/convert_element_type | solution.py:49
  213.0 4.5 %reduce.1 = bf16[128,8192]{0,1:T(8,128)(2,1)} reduce(bf16[128,1,8192]{0,2,1:T(8,128)(2,1)} %bitcast.41, bf16[]{:T(256)} %broadcast.42), dimensions={1}, to_apply=%copy.36.reduce_sub_computation | reduce | bytes 4194306 | tf_op jit(solution)/shard_map/convert_element_type | solution.py:49
  217.6 4.1 %copy.54 = bf16[128,8192]{1,0:T(8,128)(2,1)} copy(bf16[128,8192]{0,1:T(8,128)(2,1)} %reduce.1) | data formatting | bytes 4194304
  221.7 4.5 %reshape.152 = bf16[128,2,4096]{2,1,0:T(2,128)(2,1)} reshape(bf16[128,8192]{1,0:T(8,128)(2,1)} %copy.54) | data formatting | bytes 4194304
  226.2 14.3 %all-to-all-start.2 = ((bf16[128,2,4096]{2,1,0:T(2,128)(2,1)}), bf16[128,2,4096]{2,1,0:T(2,128)(2,1)}, u32[]{:S(2)}, u32[]{:S(2)}) async-start(bf16[128,2,4096]{2,1,0:T(2,128)(2,1)} %reshape.152), calls=%async_computation.2 | async-start | bytes 4194304 | tf_op jit(solution)/shard_map/all_to_all | solution.py:48
  240.5 3.3 copy.38
  243.8 9.3 %fusion.5 = f32[192,128,64]{1,2,0:T(8,128)} fusion(bf16[192,128,64]{1,2,0:T(8,128)(2,1)S(1)} %gather_fusion.4, bf16[192,128,128]{2,1,0:T(8,128)(2,1)} %param.12, bf16[192,128,128]{2,1,0:T(8,128)(2,1)} %all-reduce.2.cloned.1.call-done, f32[192,128]{1,0:T(8,128)S(1)} %gather_fusion.2, f32[192,128]{1,0:T(8,128)S(1)} %gather_fusion.1), kind=kOutput, calls=%fused_computation.18 | convolution fusion | flops 421527552 | bytes 22216704 | tf_op jit(solution)/shard_map/bij,bik->bjk/dot_general | solution.py:43
  253.1 0.1 broadcast_in_dim.31
  253.2 20.0 %scatter_fusion.1 = f32[32,128,64]{1,2,0:T(8,128)S(1)} fusion(f32[32,128,64]{1,2,0:T(8,128)S(1)} %broadcast_in_dim.31, s32[192]{0:T(256)S(1)} %compare_select_fusion, f32[192,128,64]{1,2,0:T(8,128)} %fusion.5), kind=kCustom, calls=%fused_computation.8 | custom fusion | flops 1572864 | bytes 18875136 | tf_op jit(solution)/shard_map/scatter-add | solution.py:47
  273.2 1.1 fusion.4
  274.3 15.0 %all-to-all-done.2 = bf16[128,2,4096]{2,1,0:T(2,128)(2,1)} async-done(((bf16[128,2,4096]{2,1,0:T(2,128)(2,1)}), bf16[128,2,4096]{2,1,0:T(2,128)(2,1)}, u32[]{:S(2)}, u32[]{:S(2)}) %all-to-all-start.2) | async-done | bytes 2097184 | tf_op jit(solution)/shard_map/all_to_all | solution.py:48
  289.4 13.8 %reshape.153 = bf16[128,1,8192]{2,1,0:T(2,128)(2,1)} reshape(bf16[128,2,4096]{2,1,0:T(2,128)(2,1)} %all-to-all-done.2) | data formatting | bytes 4194304
  303.2 12.3 %reshape.65 = f32[128,1,8192]{2,1,0:T(1,128)} convert(bf16[128,1,8192]{2,1,0:T(2,128)(2,1)} %reshape.153) | non-fusion elementwise | flops 1048576 | bytes 6291456 | tf_op jit(solution)/shard_map/reshape | solution.py:57
  315.5 11.1 %scatter_custom_fusion.1 = f32[48,8192]{1,0:T(8,128)} fusion(s32[128]{0:T(128)S(1)} %fusion.9, f32[128,1,8192]{2,1,0:T(1,128)} %reshape.65, f32[]{:T(128)} %constant.8.clone.1), kind=kCustom, calls=%fused_computation.10 | custom fusion | flops 1048576 | bytes 5767172 | tf_op jit(solution)/shard_map/scatter-add | solution.py:56
  326.6 3.5 %reshape.62 = f32[6144,64]{1,0:T(8,128)} reshape(f32[48,8192]{1,0:T(8,128)} %scatter_custom_fusion.1) | data formatting | bytes 3145728 | tf_op jit(solution)/shard_map/reshape | solution.py:59
  330.1 4.0 %multiply_subtract_fusion = f32[6144,64]{1,0:T(8,128)} fusion(f32[6144,64]{1,0:T(8,128)S(1)} %copy-done, f32[6144,64]{1,0:T(8,128)} %reshape.62), kind=kLoop, calls=%fused_computation.14 | loop fusion | flops 1572864 | bytes 4718592 | tf_op jit(solution)/shard_map/sub | solution.py:59
  334.2 3.2 copy.40
  (19 shorter events, 0.1 us)
Async XLA Ops:
  21.2 20.9 %copy-start.4 = (s32[192]{0:T(256)S(1)}, s32[192]{0:T(256)}, u32[]{:S(2)}) copy-start(s32[192]{0:T(256)} %param.15) | copy-start | bytes 2308
  25.7 65.6 %all-to-all-start.1 = ((bf16[128,2,4096]{2,1,0:T(2,128)(2,1)}), bf16[128,2,4096]{2,1,0:T(2,128)(2,1)S(1)}, u32[]{:S(2)}, u32[]{:S(2)}) async-start(bf16[128,2,4096]{2,1,0:T(2,128)(2,1)} %reshape.150), calls=%async_computation.1 | async-start | bytes 4194304 | tf_op jit(solution)/shard_map/all_to_all | solution.py:30
  42.0 119.0 %all-reduce.2.cloned.1.call-start = ((), (), s32[]{:S(2)}) async-start(), calls=%async_computation.3 | async-start | bytes 12582912 | tf_op jit(solution)/shard_map/psum | solution.py:40
  43.4 2.7 copy-start.5
  119.4 0.7 copy-start.2
  119.4 12.1 %copy-start.3 = (s32[4096]{0:T(1024)S(1)}, s32[4096]{0:T(1024)}, u32[]{:S(2)}) copy-start(s32[4096]{0:T(1024)} %param.11) | copy-start | bytes 49156
  121.6 20.3 %all-to-all-start = ((bf16[128,1,128]{2,1,0:T(2,128)(2,1)}), bf16[128,1,128]{2,1,0:T(2,128)(2,1)S(1)}, u32[]{:S(2)}, u32[]{:S(2)}) async-start(bf16[128,1,128]{2,1,0:T(2,128)(2,1)} %copy.27), calls=%async_computation | async-start | bytes 131072 | tf_op jit(solution)/shard_map/all_to_all | solution.py:31
  226.2 63.2 %all-to-all-start.2 = ((bf16[128,2,4096]{2,1,0:T(2,128)(2,1)}), bf16[128,2,4096]{2,1,0:T(2,128)(2,1)}, u32[]{:S(2)}, u32[]{:S(2)}) async-start(bf16[128,2,4096]{2,1,0:T(2,128)(2,1)} %reshape.152), calls=%async_computation.2 | async-start | bytes 4194304 | tf_op jit(solution)/shard_map/all_to_all | solution.py:48
  253.2 20.0 %copy-start.1 = (f32[4096,64]{0,1:T(8,128)S(1)}, f32[4096,64]{0,1:T(8,128)}, u32[]{:S(2)}) copy-start(f32[4096,64]{0,1:T(8,128)} %param.9) | copy-start | bytes 3145732
  315.5 14.6 %copy-start = (f32[6144,64]{1,0:T(8,128)S(1)}, f32[6144,64]{1,0:T(8,128)}, u32[]{:S(2)}) copy-start(f32[6144,64]{1,0:T(8,128)} %copy.38) | copy-start | bytes 4718596
Sparse Core Ops, SparseCore 0:
  119.6 41.3 all-reduce.1
where the time goes:
time: 348 us; the launch traced here: 344 us
  other arithmetic  94.5 us (27%)
  waiting for transfers between devices  88.1 us (25%)
  local copies, waits for them, and re-layouts  79.9 us (23%)
  starting transfers between devices  40.6 us (12%)
  matrix products  26.8 us (8%)
  between operations  14.2 us (4%)
    all_to_all x1, waiting for transfers between devices, body(): lax.all_to_all(sent_rows, 'gx', split_axis=0, concat_axis=0, tiled=True)  45.1 us
    unnamed x20, local copies, waits for them, and re-layouts  43.9 us
    scatter-add x1, other arithmetic, body(): jnp.zeros((received, blk_rows, half_cols), jnp.float32).at[slot_of_block]  29.9 us
    scatter-add x1, other arithmetic, body(): jnp.zeros(id_bf.shape, jnp.float32).at[id_of_block].add(grad_right)  20 us
    psum x1, waiting for transfers between devices, body(): summed = lax.psum(partial_value, 'gy').astype(jnp.float32)  18.4 us
    all_to_all x1, starting transfers between devices, body(): lax.all_to_all(sent_rows, 'gx', split_axis=0, concat_axis=0, tiled=True)  16.3 us
    all_to_all x1, waiting for transfers between devices, body(): lax.all_to_all(slot_grad.reshape(peers, slot_count, blk_rows * half_cols)...  15 us
    all_to_all x1, starting transfers between devices, body(): lax.all_to_all(slot_grad.reshape(peers, slot_count, blk_rows * half_cols)...  14.3 us
  transfers between devices with their start and end apart: 4, of which 4 were waited for; matrix products, arithmetic and copies ran while one was open for 12% of the time, Pallas kernels for 0%

commit v1 on v0

v1 whole, which is shorter than its diff:
```python
import functools

import jax
import jax.numpy as jnp
from jax import lax
from jax.experimental import pallas as pl
from jax.experimental.pallas import tpu as pltpu
from jax.sharding import PartitionSpec as P

F32, BF16 = jnp.float32, jnp.bfloat16
STEP = 0.05
DECAY = 0.1
VMEM = pl.BlockSpec(memory_space=pltpu.VMEM)
SMEM = pl.BlockSpec(memory_space=pltpu.SMEM)
PARAMS = pltpu.CompilerParams(vmem_limit_bytes=48 << 20)


def count_weight(count):
    return jnp.log(1.0 + count.astype(F32)) / jnp.log(F32(1001.0))


def low_lanes(half):
    lane = lax.broadcasted_iota(jnp.int32, (1, 2 * half), 1)
    return lane < half


def split_kernel(core_ref, rec_ref, id_ref, keep_ref, send_ref, id_out_ref):
    core = core_ref[0]
    pairs, _, blk = keep_ref.shape
    low = low_lanes(blk // 2)

    def pair(m, _):
        first = rec_ref[:, pl.ds(pl.multiple_of(m * 2 * blk, blk), blk)]
        second = rec_ref[:, pl.ds(pl.multiple_of(m * 2 * blk + blk, blk), blk)]
        half0 = jnp.where(low, first, pltpu.roll(second, blk // 2, 1))
        half1 = jnp.where(low, pltpu.roll(first, blk // 2, 1), second)
        keep_ref[m] = jnp.where(core == 0, half0, half1).astype(BF16)
        send_ref[m] = jnp.where(core == 0, half1, half0).astype(BF16)
        return 0

    lax.fori_loop(0, pairs, pair, 0, unroll=2)
    for n in range(id_out_ref.shape[0]):
        id_out_ref[n] = id_ref[:, n * blk : (n + 1) * blk].astype(BF16)


def pack_kernel(core_ref, list_ref, keep_ref, recv_ref, count_ref, out_ref, weight_ref, blocks, weights):
    core = core_ref[0]
    pairs, half_cols, blk = keep_ref.shape
    half = blk // 2

    def pair(m, _):
        keep, recv = keep_ref[m].astype(F32), recv_ref[m].astype(F32)
        low = jnp.where(core == 0, keep, recv)
        high = jnp.where(core == 0, recv, keep)
        rows = jnp.concatenate([low, high], axis=0).T.astype(BF16)
        blocks[2 * m] = rows[:half]
        blocks[2 * m + 1] = rows[half:]
        return 0

    lax.fori_loop(0, pairs, pair, 0, unroll=2)
    weight = count_weight(count_ref[...])
    weights[...] = jnp.where(core == 0, weight, pltpu.roll(weight, half, 1))

    def chunk(e, _):
        r = list_ref[e]
        out_ref[e] = blocks[r]
        weight_ref[pl.ds(e, 1), :] = weights[pl.ds(r, 1), :]
        return 0

    lax.fori_loop(0, out_ref.shape[0], chunk, 0, unroll=8)


def ident_kernel(core_ref, own_ref, peer_ref, count_ref, idt_ref, id_ref, weight_ref):
    core = core_ref[0]

    def block(n, _):
        own, peer = own_ref[n].astype(F32), peer_ref[n].astype(F32)
        low = jnp.where(core == 0, own, peer)
        high = jnp.where(core == 0, peer, own)
        full = jnp.concatenate([low, high], axis=0)
        idt_ref[n] = full.astype(BF16)
        id_ref[n] = full.T.astype(BF16)
        return 0

    lax.fori_loop(0, own_ref.shape[0], block, 0, unroll=2)
    weight_ref[...] = count_weight(count_ref[...])


def score_kernel(
    core_ref, slot_ref, ident_ref, rows_ref, idt_ref, id_ref, weight_ref, obs_ref, resid_ref, out_ref, grad
):
    step = pl.program_id(0)
    group = obs_ref.shape[0]

    @pl.when(step == 0)
    def _():
        grad[...] = jnp.zeros_like(grad)

    parts = []
    for u in range(group):
        b = step * group + u
        s, n = slot_ref[b], ident_ref[b]
        score = jnp.dot(rows_ref[s], idt_ref[n], preferred_element_type=F32)
        resid = (weight_ref[pl.ds(n, 1), :] * (score - obs_ref[u].astype(F32))).astype(BF16)
        resid_ref[u] = resid
        parts.append((s, jnp.dot(resid, id_ref[n], preferred_element_type=F32)))
    for s, part in parts:
        grad[s] += part

    @pl.when(step == pl.num_programs(0) - 1)
    def _():
        out_ref[...] = grad[...].astype(BF16)


def ident_grad_kernel(core_ref, slot_ref, ident_ref, rows_ref, weight_ref, resid_ref, keep_ref, send_ref, grad, turned):
    step = pl.program_id(0)
    group = resid_ref.shape[0]
    half = resid_ref.shape[1]
    core = core_ref[0]

    @pl.when(step == 0)
    def _():
        grad[...] = jnp.zeros_like(grad)

        def turn(s, _):
            rows = rows_ref[s].astype(F32).T
            turned[s] = (rows * weight_ref[pl.ds(s, 1), :half]).astype(BF16)
            return 0

        lax.fori_loop(0, rows_ref.shape[0], turn, 0, unroll=4)

    parts = []
    for u in range(group):
        b = step * group + u
        s, n = slot_ref[b], ident_ref[b]
        parts.append((n, jnp.dot(turned[s], resid_ref[u], preferred_element_type=F32)))
    for n, part in parts:
        grad[n] += part

    @pl.when(step == pl.num_programs(0) - 1)
    def _():
        for n in range(grad.shape[0]):
            own = pl.multiple_of(core * half, half)
            other = pl.multiple_of((1 - core) * half, half)
            keep_ref[n] = grad[n, pl.ds(own, half), :]
            send_ref[n] = grad[n, pl.ds(other, half), :]


def ident_update_kernel(id_ref, own_ref, peer_ref, out_ref):
    blk = own_ref.shape[2]
    for n in range(own_ref.shape[0]):
        old = id_ref[:, n * blk : (n + 1) * blk]
        grad = own_ref[n] + peer_ref[n]
        out_ref[:, n * blk : (n + 1) * blk] = old - STEP * (grad + DECAY * old)


def collect_kernel(core_ref, list_ref, back_ref, count_ref, keep_ref, send_ref, grad, weights):
    core = core_ref[0]
    pairs, half_cols, blk = keep_ref.shape
    half = blk // 2
    grad[...] = jnp.zeros_like(grad)
    weight = count_weight(count_ref[...]).astype(BF16).astype(F32)
    weights[...] = jnp.where(core == 0, weight, pltpu.roll(weight, half, 1))

    def add(e, _):
        r = list_ref[e]
        grad[r] += back_ref[e].astype(F32)
        return 0

    lax.fori_loop(0, back_ref.shape[0], add, 0, unroll=8)
    low = low_lanes(half)

    def pair(m, _):
        both = jnp.concatenate([grad[2 * m], grad[2 * m + 1]], axis=0).T
        row = jnp.where(low, weights[pl.ds(2 * m, 1), :], pltpu.roll(weights[pl.ds(2 * m + 1, 1), :], half, 1))
        both = both * row
        first, last = both[:half_cols], both[half_cols:]
        keep_ref[m] = jnp.where(core == 0, first, last)
        send_ref[m] = jnp.where(core == 0, last, first)
        return 0

    lax.fori_loop(0, pairs, pair, 0, unroll=2)


def record_update_kernel(core_ref, rec_ref, keep_ref, recv_ref, out_ref):
    core = core_ref[0]
    pairs, _, blk = keep_ref.shape
    low = low_lanes(blk // 2)

    def pair(m, _):
        keep, recv = keep_ref[m], recv_ref[m]
        half0 = jnp.where(core == 0, keep, recv)
        half1 = jnp.where(core == 0, recv, keep)
        grads = (
            jnp.where(low, half0, pltpu.roll(half1, blk // 2, 1)),
            jnp.where(low, pltpu.roll(half0, blk // 2, 1), half1),
        )
        for k, grad in enumerate(grads):
            at = pl.ds(pl.multiple_of(m * 2 * blk + k * blk, blk), blk)
            old = rec_ref[:, at]
            out_ref[:, at] = old - STEP * (grad + DECAY * old)
        return 0

    lax.fori_loop(0, pairs, pair, 0, unroll=2)


def call(kernel, outs, ins, scratch=(), name=None):
    return pl.pallas_call(
        kernel,
        out_shape=[jax.ShapeDtypeStruct(s, t) for s, t in outs],
        in_specs=ins,
        out_specs=[VMEM] * len(outs),
        scratch_shapes=[pltpu.VMEM(s, t) for s, t in scratch],
        compiler_params=PARAMS,
        name=name,
    )


def body(records, idents, rec_count, id_count, observed, send_list, slot_of_block, id_of_block):
    peers = lax.axis_size("gx")
    core = lax.axis_index("gy").astype(jnp.int32).reshape(1)
    blocks, blk = observed.shape[0], observed.shape[1]
    half_cols = records.shape[1]
    rank = 2 * half_cols
    half = blk // 2
    recs, ids = records.shape[0] // blk, idents.shape[0] // blk
    pairs = recs // 2
    rec_t, id_t = records.T, idents.T
    sends = send_list.reshape(-1)
    rec_count, id_count = rec_count.reshape(recs, blk), id_count.reshape(ids, blk)
    swap = functools.partial(lax.ppermute, axis_name="gy", perm=[(0, 1), (1, 0)])
    exchange = functools.partial(lax.all_to_all, axis_name="gx", split_axis=0, concat_axis=0, tiled=True)

    half_shape = (pairs, half_cols, blk)
    keep, send, id_half = call(
        split_kernel,
        [(half_shape, BF16), (half_shape, BF16), ((ids, half_cols, blk), BF16)],
        [SMEM, VMEM, VMEM],
        name="split",
    )(core, rec_t, id_t)
    recv = swap(send)
    chunks, chunk_weight = call(
        pack_kernel,
        [((peers, half, rank), BF16), ((peers, blk), F32)],
        [SMEM, SMEM, VMEM, VMEM, VMEM],
        [((recs, half, rank), BF16), ((recs, blk), F32)],
        name="pack",
    )(core, sends, keep, recv, rec_count)
    arrived_weight = exchange(chunk_weight.astype(BF16).reshape(peers, 1, blk)).reshape(peers, blk).astype(F32)
    arrived = exchange(chunks)

    id_peer = swap(id_half)
    idt, id_rows, id_weight = call(
        ident_kernel,
        [((ids, rank, blk), BF16), ((ids, blk, rank), BF16), ((ids, blk), F32)],
        [SMEM, VMEM, VMEM, VMEM],
        name="ident",
    )(core, id_half, id_peer, id_count)

    group = 8

    def whole(shape):
        return pl.BlockSpec(shape, lambda *_: (0,) * len(shape))

    resid, slot_grad = pl.pallas_call(
        score_kernel,
        out_shape=[
            jax.ShapeDtypeStruct((blocks, half, blk), BF16),
            jax.ShapeDtypeStruct((peers, half, rank), BF16),
        ],
        grid_spec=pltpu.PrefetchScalarGridSpec(
            num_scalar_prefetch=3,
            grid=(blocks // group,),
            in_specs=[
                whole((peers, half, rank)),
                whole((ids, rank, blk)),
                whole((ids, blk, rank)),
                whole((ids, blk)),
                pl.BlockSpec((group, half, blk), lambda i, core, *_: (i, core[0], 0)),
            ],
            out_specs=[pl.BlockSpec((group, half, blk), lambda i, *_: (i, 0, 0)), whole((peers, half, rank))],
            scratch_shapes=[pltpu.VMEM((peers, half, rank), F32)],
        ),
        compiler_params=PARAMS,
        name="score",
    )(core, slot_of_block, id_of_block, arrived, idt, id_rows, id_weight, observed)
    returned = exchange(slot_grad)

    id_keep, id_send = pl.pallas_call(
        ident_grad_kernel,
        out_shape=[jax.ShapeDtypeStruct((ids, half_cols, blk), F32)] * 2,
        grid_spec=pltpu.PrefetchScalarGridSpec(
            num_scalar_prefetch=3,
            grid=(blocks // group,),
            in_specs=[
                whole((peers, half, rank)),
                whole((peers, blk)),
                pl.BlockSpec((group, half, blk), lambda i, *_: (i, 0, 0)),
            ],
            out_specs=[whole((ids, half_cols, blk))] * 2,
            scratch_shapes=[pltpu.VMEM((ids, rank, blk), F32), pltpu.VMEM((peers, rank, half), BF16)],
        ),
        compiler_params=PARAMS,
        name="ident_grad",
    )(core, slot_of_block, id_of_block, arrived, arrived_weight, resid)
    id_recv = swap(id_send)
    (new_id_t,) = call(ident_update_kernel, [(id_t.shape, F32)], [VMEM] * 3, name="ident_update")(
        id_t, id_keep, id_recv
    )

    rec_keep, rec_send = call(
        collect_kernel,
        [(half_shape, F32), (half_shape, F32)],
        [SMEM, SMEM, VMEM, VMEM],
        [((recs, half, rank), F32), ((recs, blk), F32)],
        name="collect",
    )(core, sends, returned, rec_count)
    rec_recv = swap(rec_send)
    (new_rec_t,) = call(record_update_kernel, [(rec_t.shape, F32)], [SMEM, VMEM, VMEM, VMEM], name="record_update")(
        core, rec_t, rec_keep, rec_recv
    )
    return new_rec_t.T, new_id_t.T


def solution(mesh):
    in_specs = (
        P("gx", "gy"),
        P("gx", "gy"),
        P("gx"),
        P("gx"),
        P("gx", None, None),
        P("gx", None),
        P("gx"),
        P("gx"),
    )
    out_specs = (P("gx", "gy"), P("gx", "gy"))
    return jax.shard_map(body, mesh=mesh, in_specs=in_specs, out_specs=out_specs, check_vma=False)
```

time: 348 us -> 185 us (0.53)
  other arithmetic: 94.5 us -> 0.01 us
  local copies, waits for them, and re-layouts: 79.9 us -> 6.08 us
  Pallas kernels: 0 us -> 51 us
  matrix products: 26.8 us -> 0 us
  between operations: 14.2 us -> 0.77 us
  waiting for transfers between devices: 88.1 us -> 77.7 us
  starting transfers between devices: 40.6 us -> 47.8 us
    scatter-add x3 -> x0, other arithmetic: 60.9 us -> none  [the longest x1 29.9 us: body(): jnp.zeros((received, blk_rows, half_cols), jnp.float32).at[slot_of_block]]
    pallas_call x0 -> x8, Pallas kernels: none -> 51 us  [the longest x1 19.4 us: body(): pl.pallas_call(score_kernel, out_shape=[jax.ShapeDtypeStruct((blocks, hal...]
    unnamed x20 -> x26, local copies, waits for them, and re-layouts: 43.9 us -> 5.4 us
    dot_general x3 -> x0, matrix products: 26.8 us -> none  [the longest x1 11 us: body(): jnp.einsum('bij,bjk->bik', resid, right_rows, preferred_element_type=jnp....]
    reshape x6 -> x1, other arithmetic: 19.2 us -> 0.01 us  [body(): chunk_weight.astype(BF16).reshape(peers, 1, blk)]
    psum x1 -> x0, waiting for transfers between devices: 18.4 us -> none  [body(): summed = lax.psum(partial_value, 'gy').astype(jnp.float32)]
    gather x8 -> x0, local copies, waits for them, and re-layouts: 12.6 us -> none  [the longest x2 4.39 us: body(): rec_bf[send_list].reshape(peers, slot_count, blk_rows * half_cols)]
    ppermute x0 -> x4, starting transfers between devices: none -> 10.1 us  [the longest x1 4.3 us: body(): rec_recv = swap(rec_send)]
  transfers between devices with their start and end apart: 4 -> 7, of which waited for: 4 -> 4; matrix products, arithmetic and copies ran while one was open for 12% -> 0% of each run, Pallas kernels for 0% -> 25%
where the time goes in v1:
time: 185 us; the launch traced here: 183 us
  waiting for transfers between devices  77.7 us (42%)
  Pallas kernels  51 us (28%)
  starting transfers between devices  47.8 us (26%)
  local copies, waits for them, and re-layouts  6.08 us (3%)
    all_to_all x1, waiting for transfers between devices, body(): arrived = exchange(chunks)  48 us
    all_to_all x1, waiting for transfers between devices, body(): returned = exchange(slot_grad)  27.6 us
    pallas_call x1, Pallas kernels, body(): pl.pallas_call(score_kernel, out_shape=[jax.ShapeDtypeStruct((blocks, hal...  19.4 us
    pallas_call x1, Pallas kernels, body(): pl.pallas_call(ident_grad_kernel, out_shape=[jax.ShapeDtypeStruct((ids, h...  19.2 us
    all_to_all x1, starting transfers between devices, body(): arrived = exchange(chunks)  13.9 us
    all_to_all x1, starting transfers between devices, body(): returned = exchange(slot_grad)  13.9 us
    all_to_all x1, starting transfers between devices, body(): exchange(chunk_weight.astype(BF16).reshape(peers, 1, blk))  9.97 us
    unnamed x26, local copies, waits for them, and re-layouts  5.4 us
  transfers between devices with their start and end apart: 7, of which 4 were waited for; matrix products, arithmetic and copies ran while one was open for 0% of the time, Pallas kernels for 25%

profile of v1, /device:TPU:1, one launch (start us, length us, event | category | flops | bytes accessed | tf_op | source)
XLA Modules:
  0.0 183.4 jit_solution(7033031039512313216)
XLA Ops:
  0.6 0.0 copy-start.12
  0.6 0.0 copy-start.2
  0.7 1.4 copy-done.2
  2.1 0.0 copy-start.4
  2.1 1.2 copy-done.4
  3.3 0.0 copy-start.8
  3.3 1.1 split.1
  4.4 3.3 %collective-permute-start = (bf16[24,64,128]{2,1,0:T(8,128)(2,1)S(1)}, bf16[24,64,128]{2,1,0:T(8,128)(2,1)S(1)}, u32[]{:S(2)}, u32[]{:S(2)}) collective-permute-start(bf16[24,64,128]{2,1,0:T(8,128)(2,1)S(1)} %get-tuple-element.17), channel_id=1, source_target_pairs={{0,1},{1,0},{2,3},{3,2},{4,5},{5,4},{6,7},{7,6},{8,9},{9,8},{10,11... | collective-permute-start | bytes 1179656 | tf_op jit(solution)/shard_map/ppermute | solution.py:241
  7.7 1.3 collective-permute-done.recv_ref
  9.1 0.0 copy-done.12
  9.1 0.0 copy-done.8
  9.1 2.1 %pack.1 = (bf16[128,64,128]{2,1,0:T(8,128)(2,1)S(1)}, f32[128,128]{1,0:T(8,128)S(1)}) custom-call(s32[1]{0:T(128)} %bitcast.core_ref, s32[128]{0:T(128)S(1)} %bitcast.20, bf16[24,64,128]{2,1,0:T(8,128)(2,1)S(1)} %get-tuple-element.16.keep_ref, bf16[24,64,128]{2,1,0:T(8,128)(2,1)S(1)} %collective-permute-done.recv_ref, s32[48,128]{1,0:T(8,128)S(1)} %bitcast.17), custom_call_target="tpu_custom_call" | custom-call | tf_op jit(solution)/shard_map/pack/pallas_call | solution.py:242
  11.2 0.0 copy-start.7
  11.3 1.3 copy-done.7
  12.6 0.0 copy-start.9
  12.6 0.0 copy-start.10
  12.6 0.0 copy-start.11
  12.6 13.9 %all-to-all-start = ((bf16[128,64,128]{2,1,0:T(8,128)(2,1)}), bf16[128,64,128]{2,1,0:T(8,128)(2,1)S(1)}, u32[]{:S(2)}, u32[]{:S(2)}) async-start(bf16[128,64,128]{2,1,0:T(8,128)(2,1)} %copy-done.7), calls=%async_computation | async-start | bytes 4194304 | tf_op jit(solution)/shard_map/all_to_all | solution.py:250
  26.5 0.7 collective-permute-start.1
  27.3 0.7 copy.10
  27.9 48.0 %all-to-all-done.rows_ref = bf16[128,64,128]{2,1,0:T(8,128)(2,1)S(1)} async-done(((bf16[128,64,128]{2,1,0:T(8,128)(2,1)}), bf16[128,64,128]{2,1,0:T(8,128)(2,1)S(1)}, u32[]{:S(2)}, u32[]{:S(2)}) %all-to-all-start) | async-done | bytes 2097184 | tf_op jit(solution)/shard_map/all_to_all | solution.py:250
  76.0 0.0 copy-start
  76.0 10.0 %all-to-all-start.2 = ((bf16[128,1,128]{2,1,0:T(2,128)(2,1)}), bf16[128,1,128]{2,1,0:T(2,128)(2,1)S(1)}, u32[]{:S(2)}, u32[]{:S(2)}) async-start(bf16[128,1,128]{2,1,0:T(2,128)(2,1)} %copy.10), calls=%async_computation.2 | async-start | bytes 131072 | tf_op jit(solution)/shard_map/all_to_all | solution.py:249
  86.0 0.0 collective-permute-done.1.peer_ref
  86.0 0.0 copy-done.9
  86.0 1.7 ident.1
  87.7 0.0 copy-done
  87.7 0.0 copy-done.10
  87.7 0.0 copy-done.11
  87.7 19.4 %score.1 = (bf16[192,64,128]{2,1,0:T(8,128)(2,1)}, bf16[128,64,128]{2,1,0:T(8,128)(2,1)S(1)}) custom-call(s32[1]{0:T(128)} %bitcast.core_ref, s32[192]{0:T(256)S(1)} %copy-done.10, s32[192]{0:T(256)S(1)} %copy-done.11, bf16[128,64,128]{2,1,0:T(8,128)(2,1)} %copy-done, bf16[32,128,128]{2,1,0:T(8,128)(2,1)S(1)} %get-tuple-element.20.idt_ref, ...), custom_call_target="tpu_custom_call" | custom-call | tf_op jit(solution)/shard_map/score/pallas_call | solution.py:265
  107.1 0.0 copy-start.6
  107.1 1.4 copy-done.6
  108.5 0.0 all-to-all-done.2
  108.5 13.9 %all-to-all-start.1 = ((bf16[128,64,128]{2,1,0:T(8,128)(2,1)}), bf16[128,64,128]{2,1,0:T(8,128)(2,1)}, u32[]{:S(2)}, u32[]{:S(2)}) async-start(bf16[128,64,128]{2,1,0:T(8,128)(2,1)} %copy-done.6), calls=%async_computation.1 | async-start | bytes 4194304 | tf_op jit(solution)/shard_map/all_to_all | solution.py:287
  122.4 0.0 copy-done.1
  122.4 19.2 %ident_grad.1 = (f32[32,64,128]{2,1,0:T(8,128)S(1)}, f32[32,64,128]{2,1,0:T(8,128)}) custom-call(s32[1]{0:T(128)} %bitcast.core_ref, s32[192]{0:T(256)S(1)} %copy-done.10, s32[192]{0:T(256)S(1)} %copy-done.11, bf16[128,64,128]{2,1,0:T(8,128)(2,1)S(1)} %copy-done.1, f32[128,128]{1,0:T(8,128)S(1)} %bitcast_convert_fusion.weight_ref, ...), custom_call_target="tpu_custom_call" | custom-call | tf_op jit(solution)/shard_map/ident_grad/pallas_call | solution.py:289
  141.7 0.0 copy-start.5
  141.7 1.7 collective-permute-start.3
  143.4 27.6 %all-to-all-done.1.back_ref = bf16[128,64,128]{2,1,0:T(8,128)(2,1)} async-done(((bf16[128,64,128]{2,1,0:T(8,128)(2,1)}), bf16[128,64,128]{2,1,0:T(8,128)(2,1)}, u32[]{:S(2)}, u32[]{:S(2)}) %all-to-all-start.1) | async-done | bytes 2097184 | tf_op jit(solution)/shard_map/all_to_all | solution.py:287
  171.0 3.8 %collect.1 = (f32[24,64,128]{2,1,0:T(8,128)S(1)}, f32[24,64,128]{2,1,0:T(8,128)S(1)}) custom-call(s32[1]{0:T(128)} %bitcast.core_ref, s32[128]{0:T(128)S(1)} %bitcast.21, bf16[128,64,128]{2,1,0:T(8,128)(2,1)} %all-to-all-done.1.back_ref, s32[48,128]{1,0:T(8,128)S(1)} %bitcast.18), custom_call_target="tpu_custom_call" | custom-call | tf_op jit(solution)/shard_map/collect/pallas_call | solution.py:311
  174.8 4.3 %collective-permute-start.2 = (f32[24,64,128]{2,1,0:T(8,128)S(1)}, f32[24,64,128]{2,1,0:T(8,128)S(1)}, u32[]{:S(2)}, u32[]{:S(2)}) collective-permute-start(f32[24,64,128]{2,1,0:T(8,128)S(1)} %get-tuple-element.25), channel_id=1, source_target_pairs={{0,1},{1,0},{2,3},{3,2},{4,5},{5,4},{6,7},{7,6},{8,9},{9,8},{10,11... | collective-permute-start | bytes 2359304 | tf_op jit(solution)/shard_map/ppermute | solution.py:318
  179.1 0.0 collective-permute-done.3.peer_ref
  179.1 0.0 copy-done.5
  179.1 0.0 copy-start.3
  179.1 1.2 ident_update.1
  180.2 0.7 collective-permute-done.2.recv_ref
  181.0 0.0 copy-done.3
  181.0 2.4 %record_update.1 = f32[64,6144]{1,0:T(8,128)} custom-call(s32[1]{0:T(128)} %bitcast.core_ref, f32[64,6144]{1,0:T(8,128)S(1)} %bitcast.14, f32[24,64,128]{2,1,0:T(8,128)S(1)} %get-tuple-element.24.keep_ref, f32[24,64,128]{2,1,0:T(8,128)S(1)} %collective-permute-done.2.recv_ref), custom_call_target="tpu_custom_call" | custom-call | tf_op jit(solution)/shard_map/record_update/pallas_call | solution.py:319
  (3 shorter events, 0.0 us)
Async XLA Ops:
  0.6 8.5 %copy-start.12 = (s32[128,1]{0,1:T(1,128)S(1)}, s32[128,1]{0,1:T(1,128)}, u32[]{:S(2)}) copy-start(s32[128,1]{0,1:T(1,128)} %param.13) | copy-start | bytes 1540
  0.6 1.4 copy-start.2
  2.1 1.2 copy-start.4
  3.3 5.8 %copy-start.8 = (s32[6144]{0:T(1024)S(1)}, s32[6144]{0:T(1024)}, u32[]{:S(2)}) copy-start(s32[6144]{0:T(1024)} %param.10) | copy-start | bytes 73732
  4.4 4.7 %collective-permute-start = (bf16[24,64,128]{2,1,0:T(8,128)(2,1)S(1)}, bf16[24,64,128]{2,1,0:T(8,128)(2,1)S(1)}, u32[]{:S(2)}, u32[]{:S(2)}) collective-permute-start(bf16[24,64,128]{2,1,0:T(8,128)(2,1)S(1)} %get-tuple-element.17), channel_id=1, source_target_pairs={{0,1},{1,0},{2,3},{3,2},{4,5},{5,4},{6,7},{7,6},{8,9},{9,8},{10,11... | collective-permute-start | bytes 1179656 | tf_op jit(solution)/shard_map/ppermute | solution.py:241
  11.2 1.3 copy-start.7
  12.6 73.4 %copy-start.9 = (s32[4096]{0:T(1024)S(1)}, s32[4096]{0:T(1024)}, u32[]{:S(2)}) copy-start(s32[4096]{0:T(1024)} %param.11) | copy-start | bytes 49156
  12.6 75.1 %copy-start.10 = (s32[192]{0:T(256)S(1)}, s32[192]{0:T(256)}, u32[]{:S(2)}) copy-start(s32[192]{0:T(256)} %slot_ref.3) | copy-start | bytes 2308
  12.6 75.1 %copy-start.11 = (s32[192]{0:T(256)S(1)}, s32[192]{0:T(256)}, u32[]{:S(2)}) copy-start(s32[192]{0:T(256)} %ident_ref.3) | copy-start | bytes 2308
  12.6 63.4 %all-to-all-start = ((bf16[128,64,128]{2,1,0:T(8,128)(2,1)}), bf16[128,64,128]{2,1,0:T(8,128)(2,1)S(1)}, u32[]{:S(2)}, u32[]{:S(2)}) async-start(bf16[128,64,128]{2,1,0:T(8,128)(2,1)} %copy-done.7), calls=%async_computation | async-start | bytes 4194304 | tf_op jit(solution)/shard_map/all_to_all | solution.py:250
  26.5 59.4 %collective-permute-start.1 = (bf16[32,64,128]{2,1,0:T(8,128)(2,1)S(1)}, bf16[32,64,128]{2,1,0:T(8,128)(2,1)S(1)}, u32[]{:S(2)}, u32[]{:S(2)}) collective-permute-start(bf16[32,64,128]{2,1,0:T(8,128)(2,1)S(1)} %get-tuple-element.19.own_ref), channel_id=1, source_target_pairs={{0,1},{1,0},{2,3},{3,2},{4,5},{5,4},{6,7},{7,6},{8,9},{9,8},{10,11... | collective-permute-start | bytes 1572872 | tf_op jit(solution)/shard_map/ppermute | solution.py:252
  76.0 11.7 %copy-start = (bf16[128,64,128]{2,1,0:T(8,128)(2,1)}, bf16[128,64,128]{2,1,0:T(8,128)(2,1)S(1)}, u32[]{:S(2)}) copy-start(bf16[128,64,128]{2,1,0:T(8,128)(2,1)S(1)} %all-to-all-done.rows_ref) | copy-start | bytes 6291460
  76.0 32.5 %all-to-all-start.2 = ((bf16[128,1,128]{2,1,0:T(2,128)(2,1)}), bf16[128,1,128]{2,1,0:T(2,128)(2,1)S(1)}, u32[]{:S(2)}, u32[]{:S(2)}) async-start(bf16[128,1,128]{2,1,0:T(2,128)(2,1)} %copy.10), calls=%async_computation.2 | async-start | bytes 131072 | tf_op jit(solution)/shard_map/all_to_all | solution.py:249
  107.1 1.4 copy-start.6
  108.5 13.9 %copy-start.1 = (bf16[128,64,128]{2,1,0:T(8,128)(2,1)S(1)}, bf16[128,64,128]{2,1,0:T(8,128)(2,1)}, u32[]{:S(2)}) copy-start(bf16[128,64,128]{2,1,0:T(8,128)(2,1)} %copy-done) | copy-start | bytes 6291460
  108.5 62.5 %all-to-all-start.1 = ((bf16[128,64,128]{2,1,0:T(8,128)(2,1)}), bf16[128,64,128]{2,1,0:T(8,128)(2,1)}, u32[]{:S(2)}, u32[]{:S(2)}) async-start(bf16[128,64,128]{2,1,0:T(8,128)(2,1)} %copy-done.6), calls=%async_computation.1 | async-start | bytes 4194304 | tf_op jit(solution)/shard_map/all_to_all | solution.py:287
  141.7 37.4 %copy-start.5 = (f32[4096,64]{0,1:T(8,128)S(1)}, f32[4096,64]{0,1:T(8,128)}, u32[]{:S(2)}) copy-start(f32[4096,64]{0,1:T(8,128)} %param.9) | copy-start | bytes 3145732
  141.7 37.4 %collective-permute-start.3 = (f32[32,64,128]{2,1,0:T(8,128)}, f32[32,64,128]{2,1,0:T(8,128)S(1)}, u32[]{:S(2)}, u32[]{:S(2)}) collective-permute-start(f32[32,64,128]{2,1,0:T(8,128)} %get-tuple-element.29), channel_id=1, source_target_pairs={{0,1},{1,0},{2,3},{3,2},{4,5},{5,4},{6,7},{7,6},{8,9},{9,8},{10,11... | collective-permute-start | bytes 3145736 | tf_op jit(solution)/shard_map/ppermute | solution.py:306
  174.8 6.2 %collective-permute-start.2 = (f32[24,64,128]{2,1,0:T(8,128)S(1)}, f32[24,64,128]{2,1,0:T(8,128)S(1)}, u32[]{:S(2)}, u32[]{:S(2)}) collective-permute-start(f32[24,64,128]{2,1,0:T(8,128)S(1)} %get-tuple-element.25), channel_id=1, source_target_pairs={{0,1},{1,0},{2,3},{3,2},{4,5},{5,4},{6,7},{7,6},{8,9},{9,8},{10,11... | collective-permute-start | bytes 2359304 | tf_op jit(solution)/shard_map/ppermute | solution.py:318
  179.1 1.9 %copy-start.3 = (f32[6144,64]{0,1:T(8,128)S(1)}, f32[6144,64]{0,1:T(8,128)}, u32[]{:S(2)}) copy-start(f32[6144,64]{0,1:T(8,128)} %param.8) | copy-start | bytes 4718596

commit v2 on v1

v2 whole, which is shorter than its diff:
```python
import functools

import jax
import jax.numpy as jnp
from jax import lax
from jax.experimental import pallas as pl
from jax.experimental.pallas import tpu as pltpu
from jax.sharding import PartitionSpec as P

F32, BF16 = jnp.float32, jnp.bfloat16
STEP = 0.05
DECAY = 0.1
VMEM = pl.BlockSpec(memory_space=pltpu.VMEM)
SMEM = pl.BlockSpec(memory_space=pltpu.SMEM)
HBM = pl.BlockSpec(memory_space=pltpu.HBM)
GRID = (4, 8, 4)
PARAMS = pltpu.CompilerParams(vmem_limit_bytes=24 << 20)


def count_weight(count):
    return jnp.log(1.0 + count.astype(F32)) / jnp.log(F32(1001.0))


def low_lanes(half):
    lane = lax.broadcasted_iota(jnp.int32, (1, 2 * half), 1)
    return lane < half


def split_kernel(core_ref, rec_ref, keep_ref, send_ref, rows, sems):
    core = core_ref[0]
    pairs, _, blk = keep_ref.shape
    low = low_lanes(blk // 2)
    parts = sems.shape[0]
    width = rec_ref.shape[1] // parts

    def copy(p):
        at = pl.ds(p * width, width)
        return pltpu.make_async_copy(rec_ref.at[:, at], rows.at[:, at], sems.at[p])

    for p in range(parts):
        copy(p).start()
    for m in range(pairs):
        if m % (pairs // parts) == 0:
            copy(m // (pairs // parts)).wait()
        first = rows[:, 2 * m * blk : (2 * m + 1) * blk]
        second = rows[:, (2 * m + 1) * blk : (2 * m + 2) * blk]
        half0 = jnp.where(low, first, pltpu.roll(second, blk // 2, 1))
        half1 = jnp.where(low, pltpu.roll(first, blk // 2, 1), second)
        keep_ref[m] = jnp.where(core == 0, half0, half1).astype(BF16)
        send_ref[m] = jnp.where(core == 0, half1, half0).astype(BF16)


def cast_kernel(id_ref, out_ref):
    blk = out_ref.shape[2]
    for n in range(out_ref.shape[0]):
        out_ref[n] = id_ref[:, n * blk : (n + 1) * blk].astype(BF16)


def pack_kernel(core_ref, list_ref, keep_ref, recv_ref, out_ref, blocks, chunks, sems):
    core = core_ref[0]
    pairs, half_cols, blk = keep_ref.shape
    half = blk // 2

    def pair(m, _):
        keep, recv = keep_ref[m].astype(F32), recv_ref[m].astype(F32)
        low = jnp.where(core == 0, keep, recv)
        high = jnp.where(core == 0, recv, keep)
        rows = jnp.concatenate([low, high], axis=0).T.astype(BF16)
        blocks[2 * m] = rows[:half]
        blocks[2 * m + 1] = rows[half:]
        return 0

    lax.fori_loop(0, pairs, pair, 0, unroll=4)

    def chunk(e, _):
        chunks[e] = blocks[list_ref[e]]
        return 0

    store_parts(chunks, out_ref, sems, lambda first, count: lax.fori_loop(first, first + count, chunk, 0, unroll=8))


def store_parts(scratch, out_ref, sems, fill):
    parts = sems.shape[0]
    count = scratch.shape[0] // parts
    copies = []
    for p in range(parts):
        fill(p * count, count)
        at = pl.ds(p * count, count)
        copies.append(pltpu.make_async_copy(scratch.at[at], out_ref.at[at], sems.at[p]))
        copies[-1].start()
    for copy in copies:
        copy.wait()


def weigh_kernel(core_ref, chip_ref, list_ref, count_ref, out_ref, weights):
    core = core_ref[0]
    peers, blk = out_ref.shape
    weight = count_weight(count_ref[...]).astype(BF16).astype(F32)
    weights[...] = jnp.where(core == 0, weight, pltpu.roll(weight, blk // 2, 1))

    def row(d, _):
        out_ref[pl.ds(d, 1), :] = weights[pl.ds(list_ref[combine(chip_ref[0], d, 1)], 1), :]
        return 0

    lax.fori_loop(0, peers, row, 0, unroll=8)


def coords(chip):
    n0, n1, n2 = GRID
    return lax.div(chip, n1 * n2), lax.rem(lax.div(chip, n2), n1), lax.rem(chip, n2)


def combine(chip, other, sign):
    x, y, z = (lax.rem(a + sign * b + n, n) for a, b, n in zip(coords(chip), coords(other), GRID))
    return (x * GRID[1] + y) * GRID[2] + z


def ident_kernel(core_ref, own_ref, peer_ref, count_ref, idt_ref, id_ref, weight_ref):
    core = core_ref[0]

    def block(n, _):
        own, peer = own_ref[n].astype(F32), peer_ref[n].astype(F32)
        low = jnp.where(core == 0, own, peer)
        high = jnp.where(core == 0, peer, own)
        full = jnp.concatenate([low, high], axis=0)
        idt_ref[n] = full.astype(BF16)
        id_ref[n] = full.T.astype(BF16)
        return 0

    lax.fori_loop(0, own_ref.shape[0], block, 0, unroll=2)
    weight_ref[...] = count_weight(count_ref[...])


GROUP = 16


def score_kernel(
    core_ref,
    slot_ref,
    ident_ref,
    rows_ref,
    weight_ref,
    idt_hbm,
    id_hbm,
    obs_hbm,
    resid_hbm,
    out_hbm,
    idt_ref,
    id_ref,
    obs_ref,
    resid_ref,
    grad,
    chunks,
    sems,
    in_sems,
    resid_sems,
    out_sems,
):
    blocks, half, _ = obs_ref.shape
    groups = blocks // GROUP
    rows_at = pl.ds(pl.multiple_of(core_ref[0] * half, half), half)
    tables = [
        pltpu.make_async_copy(idt_hbm, idt_ref, sems.at[0]),
        pltpu.make_async_copy(id_hbm, id_ref, sems.at[1]),
    ]

    def take(i):
        at = pl.ds(i * GROUP, GROUP)
        return pltpu.make_async_copy(obs_hbm.at[at, rows_at, :], obs_ref.at[at], in_sems.at[i])

    def give(i):
        at = pl.ds(i * GROUP, GROUP)
        return pltpu.make_async_copy(resid_ref.at[at], resid_hbm.at[at], resid_sems.at[i])

    tables[0].start()
    take(0).start()
    tables[1].start()
    for i in range(1, groups):
        take(i).start()
    grad[...] = jnp.zeros_like(grad)
    for table in tables:
        table.wait()

    def step(i, _):
        take(i).wait()
        at = [(i * GROUP + u, slot_ref[i * GROUP + u], ident_ref[i * GROUP + u]) for u in range(GROUP)]
        scores = [jnp.dot(rows_ref[s], idt_ref[n], preferred_element_type=F32) for _, s, n in at]
        resids = []
        for (b, s, n), score in zip(at, scores):
            resid = (weight_ref[pl.ds(n, 1), :] * (score - obs_ref[b].astype(F32))).astype(BF16)
            resid_ref[b] = resid
            resids.append(resid)
        parts = [jnp.dot(resid, id_ref[n], preferred_element_type=F32) for resid, (_, _, n) in zip(resids, at)]
        for (_, s, _), part in zip(at, parts):
            grad[s] += part
        give(i).start()
        return 0

    lax.fori_loop(0, groups, step, 0)

    def fill(first, count):
        at = pl.ds(first, count)
        chunks[at] = grad[at].astype(BF16)

    store_parts(chunks, out_hbm, out_sems, fill)
    for i in range(groups):
        give(i).wait()


def ident_grad_kernel(
    core_ref,
    chip_ref,
    slot_ref,
    ident_ref,
    rows_ref,
    weight_ref,
    resid_hbm,
    keep_ref,
    send_ref,
    grad,
    turned,
    resid_ref,
    sems,
):
    blocks, half, _ = resid_ref.shape
    core = core_ref[0]

    def take(i):
        at = pl.ds(i * GROUP, GROUP)
        return pltpu.make_async_copy(resid_hbm.at[at], resid_ref.at[at], sems.at[i])

    for i in range(blocks // GROUP):
        take(i).start()
    grad[...] = jnp.zeros_like(grad)

    def turn(s, _):
        rows = rows_ref[s].astype(F32).T
        weight = weight_ref[pl.ds(combine(chip_ref[0], s, -1), 1), :half]
        turned[s] = (rows * weight).astype(BF16)
        return 0

    lax.fori_loop(0, rows_ref.shape[0], turn, 0, unroll=4)

    def step(i, _):
        take(i).wait()
        at = [(i * GROUP + u, slot_ref[i * GROUP + u], ident_ref[i * GROUP + u]) for u in range(GROUP)]
        parts = [jnp.dot(turned[s], resid_ref[b], preferred_element_type=F32) for b, s, _ in at]
        for (_, _, n), part in zip(at, parts):
            grad[n] += part
        return 0

    lax.fori_loop(0, blocks // GROUP, step, 0)
    own = pl.multiple_of(core * half, half)
    other = pl.multiple_of((1 - core) * half, half)
    for n in range(grad.shape[0]):
        keep_ref[n] = grad[n, pl.ds(own, half), :]
        send_ref[n] = grad[n, pl.ds(other, half), :]


def ident_update_kernel(id_ref, own_ref, peer_ref, out_ref):
    blk = own_ref.shape[2]
    for n in range(own_ref.shape[0]):
        old = id_ref[:, n * blk : (n + 1) * blk]
        grad = own_ref[n] + peer_ref[n]
        out_ref[:, n * blk : (n + 1) * blk] = old - STEP * (grad + DECAY * old)


def collect_kernel(core_ref, list_ref, back_ref, count_ref, keep_ref, send_ref, grad, weights):
    core = core_ref[0]
    pairs, half_cols, blk = keep_ref.shape
    half = blk // 2
    grad[...] = jnp.zeros_like(grad)
    weight = count_weight(count_ref[...]).astype(BF16).astype(F32)
    weights[...] = jnp.where(core == 0, weight, pltpu.roll(weight, half, 1))

    def add(e, _):
        r = list_ref[e]
        grad[r] += back_ref[e].astype(F32)
        return 0

    lax.fori_loop(0, back_ref.shape[0], add, 0, unroll=8)
    low = low_lanes(half)

    def pair(m, _):
        both = jnp.concatenate([grad[2 * m], grad[2 * m + 1]], axis=0).T
        row = jnp.where(low, weights[pl.ds(2 * m, 1), :], pltpu.roll(weights[pl.ds(2 * m + 1, 1), :], half, 1))
        both = both * row
        first, last = both[:half_cols], both[half_cols:]
        keep_ref[m] = jnp.where(core == 0, first, last)
        send_ref[m] = jnp.where(core == 0, last, first)
        return 0

    lax.fori_loop(0, pairs, pair, 0, unroll=2)


def record_update_kernel(core_ref, rec_ref, keep_ref, recv_ref, out_ref):
    core = core_ref[0]
    pairs, _, blk = keep_ref.shape
    low = low_lanes(blk // 2)

    def pair(m, _):
        keep, recv = keep_ref[m], recv_ref[m]
        half0 = jnp.where(core == 0, keep, recv)
        half1 = jnp.where(core == 0, recv, keep)
        grads = (
            jnp.where(low, half0, pltpu.roll(half1, blk // 2, 1)),
            jnp.where(low, pltpu.roll(half0, blk // 2, 1), half1),
        )
        for k, grad in enumerate(grads):
            at = pl.ds(pl.multiple_of(m * 2 * blk + k * blk, blk), blk)
            old = rec_ref[:, at]
            out_ref[:, at] = old - STEP * (grad + DECAY * old)
        return 0

    lax.fori_loop(0, pairs, pair, 0, unroll=2)


def call(kernel, outs, ins, scratch=(), sems=(), name=None):
    return pl.pallas_call(
        kernel,
        out_shape=[pltpu.HBM(o[0], o[1]) if len(o) > 2 else jax.ShapeDtypeStruct(*o) for o in outs],
        in_specs=ins,
        out_specs=[HBM if len(o) > 2 else VMEM for o in outs],
        scratch_shapes=[pltpu.VMEM(*t) for t in scratch] + [pltpu.SemaphoreType.DMA((n,)) for n in sems],
        compiler_params=PARAMS,
        name=name,
    )


def in_hbm(x):
    return pltpu.with_memory_space_constraint(x, pltpu.HBM)


def by_offsets(rows):
    width = rows.shape[1]
    chips = GRID[0] * GRID[1] * GRID[2]
    rows = rows.reshape(*GRID, width)
    for axis, extent in enumerate(GRID):
        stride = 1
        for n in GRID[axis + 1 :]:
            stride *= n
        parts = []
        for off in range(extent):
            part = lax.index_in_dim(rows, off, axis, keepdims=False)
            if off:
                pairs = []
                for g in range(chips):
                    at = (g // stride) % extent
                    pairs.append((g, g + ((at + off) % extent - at) * stride))
                part = lax.ppermute(part, "gx", pairs)
            parts.append(part)
        rows = jnp.stack(parts, axis)
    return rows.reshape(chips, width)


def body(records, idents, rec_count, id_count, observed, send_list, slot_of_block, id_of_block):
    peers = lax.axis_size("gx")
    core = lax.axis_index("gy").astype(jnp.int32).reshape(1)
    chip = lax.axis_index("gx").astype(jnp.int32).reshape(1)
    blocks, blk = observed.shape[0], observed.shape[1]
    half_cols = records.shape[1]
    rank = 2 * half_cols
    half = blk // 2
    recs, ids = records.shape[0] // blk, idents.shape[0] // blk
    pairs = recs // 2
    rec_t, id_t = records.T, idents.T
    sends = send_list.reshape(-1)
    rec_count, id_count = rec_count.reshape(recs, blk), id_count.reshape(ids, blk)
    swap = functools.partial(lax.ppermute, axis_name="gy", perm=[(0, 1), (1, 0)])
    exchange = functools.partial(lax.all_to_all, axis_name="gx", split_axis=0, concat_axis=0, tiled=True)

    half_shape = (pairs, half_cols, blk)
    chunk_shape = (peers, half, rank)
    keep, send = call(
        split_kernel, [(half_shape, BF16)] * 2, [SMEM, HBM], [(rec_t.shape, F32)], [4], name="split"
    )(core, in_hbm(rec_t))
    recv = swap(send)
    (chunks,) = call(
        pack_kernel,
        [(chunk_shape, BF16, True)],
        [SMEM, SMEM, VMEM, VMEM],
        [((recs, half, rank), BF16), (chunk_shape, BF16)],
        [4],
        name="pack",
    )(core, sends, keep, recv)
    arrived = exchange(chunks)

    (id_half,) = call(cast_kernel, [((ids, half_cols, blk), BF16)], [VMEM], name="cast")(id_t)
    id_peer = swap(id_half)
    idt, id_rows, id_weight = call(
        ident_kernel,
        [((ids, rank, blk), BF16), ((ids, blk, rank), BF16), ((ids, blk), F32)],
        [SMEM, VMEM, VMEM, VMEM],
        name="ident",
    )(core, id_half, id_peer, id_count)
    resid_shape = (blocks, half, blk)
    groups = blocks // GROUP
    resid, slot_grad = call(
        score_kernel,
        [(resid_shape, BF16, True), (chunk_shape, BF16, True)],
        [SMEM] * 3 + [VMEM] * 2 + [HBM] * 3,
        [
            ((ids, rank, blk), BF16),
            ((ids, blk, rank), BF16),
            (resid_shape, BF16),
            (resid_shape, BF16),
            (chunk_shape, F32),
            (chunk_shape, BF16),
        ],
        [2, groups, groups, 4],
        name="score",
    )(core, slot_of_block, id_of_block, arrived, id_weight, in_hbm(idt), in_hbm(id_rows), in_hbm(observed))
    returned = exchange(slot_grad)

    (weights,) = call(
        weigh_kernel, [((peers, blk), F32)], [SMEM, SMEM, SMEM, VMEM], [((recs, blk), F32)], name="weigh"
    )(core, chip, sends, rec_count)
    weights, resid = lax.optimization_barrier((weights, resid))
    arrived_weight = by_offsets(weights)
    id_keep, id_send = call(
        ident_grad_kernel,
        [((ids, half_cols, blk), F32)] * 2,
        [SMEM] * 4 + [VMEM] * 2 + [HBM],
        [((ids, rank, blk), F32), ((peers, rank, half), BF16), (resid_shape, BF16)],
        [groups],
        name="ident_grad",
    )(core, chip, slot_of_block, id_of_block, arrived, arrived_weight, in_hbm(resid))
    id_recv = swap(id_send)
    (new_id_t,) = call(ident_update_kernel, [(id_t.shape, F32)], [VMEM] * 3, name="ident_update")(
        id_t, id_keep, id_recv
    )

    rec_keep, rec_send = call(
        collect_kernel,
        [(half_shape, F32), (half_shape, F32)],
        [SMEM, SMEM, VMEM, VMEM],
        [((recs, half, rank), F32), ((recs, blk), F32)],
        name="collect",
    )(core, sends, returned, rec_count)
    rec_recv = swap(rec_send)
    (new_rec_t,) = call(record_update_kernel, [(rec_t.shape, F32)], [SMEM, VMEM, VMEM, VMEM], name="record_update")(
        core, rec_t, rec_keep, rec_recv
    )
    return new_rec_t.T, new_id_t.T


def solution(mesh):
    in_specs = (
        P("gx", "gy"),
        P("gx", "gy"),
        P("gx"),
        P("gx"),
        P("gx", None, None),
        P("gx", None),
        P("gx"),
        P("gx"),
    )
    out_specs = (P("gx", "gy"), P("gx", "gy"))
    return jax.shard_map(body, mesh=mesh, in_specs=in_specs, out_specs=out_specs, check_vma=False)
```

time: 185 us -> 174 us (0.941)
  Pallas kernels: 51 us -> 34.2 us
  starting transfers between devices: 47.8 us -> 56.4 us
  local copies, waits for them, and re-layouts: 6.08 us -> 3.73 us
    ppermute x0 -> x13, waiting for transfers between devices: none -> 31.3 us  [by_offsets(): part = lax.ppermute(part, 'gx', pairs)]
    all_to_all x1, waiting for transfers between devices: 27.6 us -> 0.01 us  [body(): returned = exchange(slot_grad)]
    ppermute x0 -> x13, starting transfers between devices: none -> 22.8 us  [by_offsets(): part = lax.ppermute(part, 'gx', pairs)]
    pallas_call x4 -> x6, Pallas kernels: 41.9 us -> 25.1 us  [the longest x1 9.66 us: body(): call(score_kernel, [(resid_shape, BF16, True), (chunk_shape, BF16, True)]...]
    all_to_all x1 -> x0, starting transfers between devices: 9.97 us -> none  [body(): exchange(chunk_weight.astype(BF16).reshape(peers, 1, blk))]
    all_to_all x1, waiting for transfers between devices: 48 us -> 43.4 us  [body(): arrived = exchange(chunks)]
    ppermute x1, starting transfers between devices: 4.3 us -> 0.18 us  [body(): rec_recv = swap(rec_send)]
    all_to_all x1, starting transfers between devices: 13.9 us -> 10.5 us  [body(): returned = exchange(slot_grad)]
  transfers between devices with their start and end apart: 7 -> 19, of which waited for: 4 -> 12; matrix products, arithmetic and copies ran while one was open for 0% -> 0% of each run, Pallas kernels for 25% -> 10%
where the time goes in v2:
time: 174 us
  waiting for transfers between devices  78.7 us (45%)
  starting transfers between devices  56.4 us (32%)
  Pallas kernels  34.2 us (20%)
  local copies, waits for them, and re-layouts  3.73 us (2%)
    all_to_all x1, waiting for transfers between devices, body(): arrived = exchange(chunks)  43.4 us
    ppermute x13, waiting for transfers between devices, by_offsets(): part = lax.ppermute(part, 'gx', pairs)  31.3 us
    ppermute x13, starting transfers between devices, by_offsets(): part = lax.ppermute(part, 'gx', pairs)  22.8 us
    all_to_all x1, starting transfers between devices, body(): arrived = exchange(chunks)  13.9 us
    all_to_all x1, starting transfers between devices, body(): returned = exchange(slot_grad)  10.5 us
    pallas_call x1, Pallas kernels, body(): call(score_kernel, [(resid_shape, BF16, True), (chunk_shape, BF16, True)]...  9.66 us
    pallas_call x1, Pallas kernels, body(): call(ident_grad_kernel, [((ids, half_cols, blk), F32)] * 2, [SMEM] * 4 +...  8.82 us
    ppermute x1, starting transfers between devices, body(): id_recv = swap(id_send)  4.97 us
  transfers between devices with their start and end apart: 19, of which 12 were waited for; matrix products, arithmetic and copies ran while one was open for 0% of the time, Pallas kernels for 10%

profile of v2, /device:TPU:1, one launch (start us, length us, event | category | flops | bytes accessed | tf_op | source)
XLA Modules:
  0.0 174.0 jit_solution(11886408840535553291)
XLA Ops:
  0.6 1.5 split.1
  2.2 3.3 %collective-permute-start = (bf16[24,64,128]{2,1,0:T(8,128)(2,1)S(1)}, bf16[24,64,128]{2,1,0:T(8,128)(2,1)S(1)}, u32[]{:S(2)}, u32[]{:S(2)}) collective-permute-start(bf16[24,64,128]{2,1,0:T(8,128)(2,1)S(1)} %get-tuple-element.16), channel_id=1, source_target_pairs={{0,1},{1,0},{2,3},{3,2},{4,5},{5,4},{6,7},{7,6},{8,9},{9,8},{10,11... | collective-permute-start | bytes 1179656 | tf_op jit(solution)/shard_map/ppermute | solution.py:377
  5.5 1.3 collective-permute-done.recv_ref
  6.9 0.7 copy-done.8
  7.5 2.6 %pack.1 = bf16[128,64,128]{2,1,0:T(8,128)(2,1)} custom-call(s32[1]{0:T(128)} %bitcast.core_ref, s32[128]{0:T(128)S(1)} %bitcast.75, bf16[24,64,128]{2,1,0:T(8,128)(2,1)S(1)} %get-tuple-element.15.keep_ref, bf16[24,64,128]{2,1,0:T(8,128)(2,1)S(1)} %collective-permute-done.recv_ref), custom_call_target="tpu_custom_call" | custom-call | tf_op jit(solution)/shard_map/pack/pallas_call | solution.py:378
  10.2 0.0 copy-start.7
  10.2 13.9 %all-to-all-start = ((bf16[128,64,128]{2,1,0:T(8,128)(2,1)}), bf16[128,64,128]{2,1,0:T(8,128)(2,1)S(1)}, u32[]{:S(2)}, u32[]{:S(2)}) async-start(bf16[128,64,128]{2,1,0:T(8,128)(2,1)} %pack.1), calls=%async_computation | async-start | bytes 4194304 | tf_op jit(solution)/shard_map/all_to_all | solution.py:386
  24.1 0.1 cast.1.own_ref
  24.2 0.7 collective-permute-start.1
  24.9 1.5 collective-permute-done.1.peer_ref
  26.5 1.7 ident.1
  28.2 1.0 copy-done.2
  29.2 1.0 copy-done.3
  30.1 43.4 %all-to-all-done.rows_ref = bf16[128,64,128]{2,1,0:T(8,128)(2,1)S(1)} async-done(((bf16[128,64,128]{2,1,0:T(8,128)(2,1)}), bf16[128,64,128]{2,1,0:T(8,128)(2,1)S(1)}, u32[]{:S(2)}, u32[]{:S(2)}) %all-to-all-start) | async-done | bytes 2097184 | tf_op jit(solution)/shard_map/all_to_all | solution.py:386
  73.6 9.7 %score.1 = (bf16[192,64,128]{2,1,0:T(8,128)(2,1)}, bf16[128,64,128]{2,1,0:T(8,128)(2,1)}) custom-call(s32[1]{0:T(128)} %bitcast.core_ref, s32[192]{0:T(256)S(1)} %copy-done.10, s32[192]{0:T(256)S(1)} %copy-done.11, bf16[128,64,128]{2,1,0:T(8,128)(2,1)S(1)} %all-to-all-done.rows_ref, f32[32,128]{1,0:T(8,128)S(1)} %get-tuple-element.17.weight_ref, ...), custom_call_target="tpu_custom_call" | custom-call | tf_op jit(solution)/shard_map/score/pallas_call | solution.py:398
  83.3 10.5 %all-to-all-start.1 = ((bf16[128,64,128]{2,1,0:T(8,128)(2,1)}), bf16[128,64,128]{2,1,0:T(8,128)(2,1)}, u32[]{:S(2)}, u32[]{:S(2)}) async-start(bf16[128,64,128]{2,1,0:T(8,128)(2,1)} %get-tuple-element.20), calls=%async_computation.1 | async-start | bytes 4194304 | tf_op jit(solution)/shard_map/all_to_all | solution.py:413
  93.8 2.4 %weigh.1 = f32[128,128]{1,0:T(8,128)S(1)} custom-call(s32[1]{0:T(128)} %bitcast.core_ref, s32[1]{0:T(128)} %bitcast.7.chip_ref, s32[128]{0:T(128)S(1)} %bitcast.76, s32[48,128]{1,0:T(8,128)S(1)} %bitcast.72), custom_call_target="tpu_custom_call" | custom-call | tf_op jit(solution)/shard_map/weigh/pallas_call | solution.py:415
  96.2 2.3 %collective-permute-start.5 = (f32[8,4,128]{2,1,0:T(4,128)S(1)}, f32[8,4,128]{2,1,0:T(4,128)S(1)}, u32[]{:S(2)}, u32[]{:S(2)}) collective-permute-start(f32[8,4,128]{2,1,0:T(4,128)S(1)} %bitcast.89), channel_id=1, source_target_pairs={{0,192},{2,194},{4,196},{6,198},{8,200},{10,202},{12,204},{14,206}... | collective-permute-start | bytes 49160 | tf_op jit(solution)/shard_map/ppermute | solution.py:350
  98.5 0.2 collective-permute-start.4
  98.7 0.8 collective-permute-start.3
  99.5 3.9 %collective-permute-done.4 = f32[8,4,128]{2,1,0:T(4,128)S(1)} collective-permute-done((f32[8,4,128]{2,1,0:T(4,128)S(1)}, f32[8,4,128]{2,1,0:T(4,128)S(1)}, u32[]{:S(2)}, u32[]{:S(2)}) %collective-permute-start.4) | collective-permute-done | bytes 16416 | tf_op jit(solution)/shard_map/ppermute | solution.py:350
  103.3 0.1 collective-permute-done.3
  103.5 0.1 pad_maximum_fusion
  103.6 1.4 collective-permute-start.6
  105.0 1.6 collective-permute-start.7
  106.6 2.9 %collective-permute-start.8 = (f32[4,4,128]{2,0,1:T(4,128)S(1)}, f32[4,4,128]{2,0,1:T(4,128)S(1)}, u32[]{:S(2)}, u32[]{:S(2)}) collective-permute-start(f32[4,4,128]{2,0,1:T(4,128)S(1)} %get-tuple-element.36), channel_id=1, source_target_pairs={{0,24},{2,26},{4,28},{6,30},{8,32},{10,34},{12,36},{14,38},{16,40}... | collective-permute-start | bytes 24584 | tf_op jit(solution)/shard_map/ppermute | solution.py:350
  109.5 1.6 collective-permute-start.9
  111.1 2.8 %collective-permute-start.10 = (f32[4,4,128]{2,0,1:T(4,128)S(1)}, f32[4,4,128]{2,0,1:T(4,128)S(1)}, u32[]{:S(2)}, u32[]{:S(2)}) collective-permute-start(f32[4,4,128]{2,0,1:T(4,128)S(1)} %get-tuple-element.34), channel_id=1, source_target_pairs={{0,40},{2,42},{4,44},{6,46},{8,48},{10,50},{12,52},{14,54},{16,56}... | collective-permute-start | bytes 24584 | tf_op jit(solution)/shard_map/ppermute | solution.py:350
  113.9 22.9 %collective-permute-done.6 = f32[4,4,128]{2,0,1:T(4,128)S(1)} collective-permute-done((f32[4,4,128]{2,0,1:T(4,128)S(1)}, f32[4,4,128]{2,0,1:T(4,128)S(1)}, u32[]{:S(2)}, u32[]{:S(2)}) %collective-permute-start.6) | collective-permute-done | bytes 8224 | tf_op jit(solution)/shard_map/ppermute | solution.py:350
  136.8 2.2 %collective-permute-start.11 = (f32[4,4,128]{2,0,1:T(4,128)S(1)}, f32[4,4,128]{2,0,1:T(4,128)S(1)}, u32[]{:S(2)}, u32[]{:S(2)}) collective-permute-start(f32[4,4,128]{2,0,1:T(4,128)S(1)} %get-tuple-element.33), channel_id=1, source_target_pairs={{0,48},{2,50},{4,52},{6,54},{8,56},{10,58},{12,60},{14,62},{16,0},... | collective-permute-start | bytes 24584 | tf_op jit(solution)/shard_map/ppermute | solution.py:350
  139.1 0.2 collective-permute-done.7
  139.3 3.0 %collective-permute-start.12 = (f32[4,4,128]{2,0,1:T(4,128)S(1)}, f32[4,4,128]{2,0,1:T(4,128)S(1)}, u32[]{:S(2)}, u32[]{:S(2)}) collective-permute-start(f32[4,4,128]{2,0,1:T(4,128)S(1)} %get-tuple-element.32), channel_id=1, source_target_pairs={{0,56},{2,58},{4,60},{6,62},{8,0},{10,2},{12,4},{14,6},{16,8},{18,... | collective-permute-start | bytes 24584 | tf_op jit(solution)/shard_map/ppermute | solution.py:350
  142.3 0.5 collective-permute-done.9
  142.8 0.3 collective-permute-done.12
  143.1 0.1 stack.59
  143.2 3.3 %collective-permute-start.15 = (f32[4,8,128]{2,1,0:T(8,128)S(1)}, f32[4,8,128]{2,1,0:T(8,128)S(1)}, u32[]{:S(2)}, u32[]{:S(2)}) collective-permute-start(f32[4,8,128]{2,1,0:T(8,128)S(1)} %get-tuple-element.29), channel_id=1, source_target_pairs={{0,6},{2,0},{4,2},{6,4},{8,14},{10,8},{12,10},{14,12},{16,22},{18,... | collective-permute-start | bytes 49160 | tf_op jit(solution)/shard_map/ppermute | solution.py:350
  146.5 0.7 collective-permute-start.13
  147.1 0.2 collective-permute-done.15
  147.3 3.2 %collective-permute-done.14 = f32[4,8,128]{2,1,0:T(8,128)S(1)} collective-permute-done((f32[4,8,128]{2,1,0:T(8,128)S(1)}, f32[4,8,128]{2,1,0:T(8,128)S(1)}, u32[]{:S(2)}, u32[]{:S(2)}) %collective-permute-start.14) | collective-permute-done | bytes 16416 | tf_op jit(solution)/shard_map/ppermute | solution.py:350
  150.6 0.1 pad_maximum_fusion.1
  150.6 8.8 %ident_grad.1 = (f32[32,64,128]{2,1,0:T(8,128)S(1)}, f32[32,64,128]{2,1,0:T(8,128)}) custom-call(s32[1]{0:T(128)} %bitcast.core_ref, s32[1]{0:T(128)} %bitcast.7.chip_ref, s32[192]{0:T(256)S(1)} %copy-done.10, s32[192]{0:T(256)S(1)} %copy-done.11, bf16[128,64,128]{2,1,0:T(8,128)(2,1)S(1)} %all-to-all-done.rows_ref, f32[128,128]{1,0:T(8,128)S(1)} %bitcast.71, ...), custom_call_target="tpu_custom_call" | custom-call | tf_op jit(solution)/shard_map/ident_grad/pallas_call | solution.py:420
  159.5 1.0 copy-done.4
  160.4 5.0 %collective-permute-start.16 = (f32[32,64,128]{2,1,0:T(8,128)}, f32[32,64,128]{2,1,0:T(8,128)S(1)}, u32[]{:S(2)}, u32[]{:S(2)}) collective-permute-start(f32[32,64,128]{2,1,0:T(8,128)} %get-tuple-element.27), channel_id=1, source_target_pairs={{0,1},{1,0},{2,3},{3,2},{4,5},{5,4},{6,7},{7,6},{8,9},{9,8},{10,11... | collective-permute-start | bytes 3145736 | tf_op jit(solution)/shard_map/ppermute | solution.py:428
  165.4 3.8 %collect.1 = (f32[24,64,128]{2,1,0:T(8,128)S(1)}, f32[24,64,128]{2,1,0:T(8,128)S(1)}) custom-call(s32[1]{0:T(128)} %bitcast.core_ref, s32[128]{0:T(128)S(1)} %bitcast.77, bf16[128,64,128]{2,1,0:T(8,128)(2,1)} %all-to-all-done.1.back_ref, s32[48,128]{1,0:T(8,128)S(1)} %bitcast.73), custom_call_target="tpu_custom_call" | custom-call | tf_op jit(solution)/shard_map/collect/pallas_call | solution.py:433
  169.2 0.2 collective-permute-start.2
  169.4 1.2 ident_update.1
  170.6 1.0 collective-permute-done.2.recv_ref
  171.6 2.4 %record_update.1 = f32[64,6144]{1,0:T(8,128)} custom-call(s32[1]{0:T(128)} %bitcast.core_ref, f32[64,6144]{1,0:T(8,128)S(1)} %bitcast.68, f32[24,64,128]{2,1,0:T(8,128)S(1)} %get-tuple-element.21.keep_ref, f32[24,64,128]{2,1,0:T(8,128)S(1)} %collective-permute-done.2.recv_ref), custom_call_target="tpu_custom_call" | custom-call | tf_op jit(solution)/shard_map/record_update/pallas_call | solution.py:441
  (30 shorter events, 0.1 us)
Async XLA Ops:
  2.2 4.7 %collective-permute-start = (bf16[24,64,128]{2,1,0:T(8,128)(2,1)S(1)}, bf16[24,64,128]{2,1,0:T(8,128)(2,1)S(1)}, u32[]{:S(2)}, u32[]{:S(2)}) collective-permute-start(bf16[24,64,128]{2,1,0:T(8,128)(2,1)S(1)} %get-tuple-element.16), channel_id=1, source_target_pairs={{0,1},{1,0},{2,3},{3,2},{4,5},{5,4},{6,7},{7,6},{8,9},{9,8},{10,11... | collective-permute-start | bytes 1179656 | tf_op jit(solution)/shard_map/ppermute | solution.py:377
  6.9 0.7 copy-start.8
  10.2 14.0 %copy-start.1 = (f32[4096,64]{0,1:T(8,128)S(1)}, f32[4096,64]{0,1:T(8,128)}, u32[]{:S(2)}) copy-start(f32[4096,64]{0,1:T(8,128)} %param.9) | copy-start | bytes 3145732
  10.2 16.3 %copy-start.7 = (s32[4096]{0:T(1024)S(1)}, s32[4096]{0:T(1024)}, u32[]{:S(2)}) copy-start(s32[4096]{0:T(1024)} %param.11) | copy-start | bytes 49156
  10.2 63.4 %all-to-all-start = ((bf16[128,64,128]{2,1,0:T(8,128)(2,1)}), bf16[128,64,128]{2,1,0:T(8,128)(2,1)S(1)}, u32[]{:S(2)}, u32[]{:S(2)}) async-start(bf16[128,64,128]{2,1,0:T(8,128)(2,1)} %pack.1), calls=%async_computation | async-start | bytes 4194304 | tf_op jit(solution)/shard_map/all_to_all | solution.py:386
  24.1 49.5 %copy-start.10 = (s32[192]{0:T(256)S(1)}, s32[192]{0:T(256)}, u32[]{:S(2)}) copy-start(s32[192]{0:T(256)} %slot_ref.3) | copy-start | bytes 2308
  24.1 49.5 %copy-start.11 = (s32[192]{0:T(256)S(1)}, s32[192]{0:T(256)}, u32[]{:S(2)}) copy-start(s32[192]{0:T(256)} %ident_ref.3) | copy-start | bytes 2308
  24.2 2.3 %collective-permute-start.1 = (bf16[32,64,128]{2,1,0:T(8,128)(2,1)S(1)}, bf16[32,64,128]{2,1,0:T(8,128)(2,1)S(1)}, u32[]{:S(2)}, u32[]{:S(2)}) collective-permute-start(bf16[32,64,128]{2,1,0:T(8,128)(2,1)S(1)} %cast.1.own_ref), channel_id=1, source_target_pairs={{0,1},{1,0},{2,3},{3,2},{4,5},{5,4},{6,7},{7,6},{8,9},{9,8},{10,11... | collective-permute-start | bytes 1572872 | tf_op jit(solution)/shard_map/ppermute | solution.py:389
  28.2 1.0 copy-start.2
  29.2 1.0 copy-start.3
  83.2 10.6 %copy-start.6 = (s32[6144]{0:T(1024)S(1)}, s32[6144]{0:T(1024)}, u32[]{:S(2)}) copy-start(s32[6144]{0:T(1024)} %param.10) | copy-start | bytes 73732
  83.3 10.5 %copy-start.9 = (s32[128,1]{0,1:T(1,128)S(1)}, s32[128,1]{0,1:T(1,128)}, u32[]{:S(2)}) copy-start(s32[128,1]{0,1:T(1,128)} %param.13) | copy-start | bytes 1540
  83.3 82.1 %all-to-all-start.1 = ((bf16[128,64,128]{2,1,0:T(8,128)(2,1)}), bf16[128,64,128]{2,1,0:T(8,128)(2,1)}, u32[]{:S(2)}, u32[]{:S(2)}) async-start(bf16[128,64,128]{2,1,0:T(8,128)(2,1)} %get-tuple-element.20), calls=%async_computation.1 | async-start | bytes 4194304 | tf_op jit(solution)/shard_map/all_to_all | solution.py:413
  96.2 3.3 %collective-permute-start.5 = (f32[8,4,128]{2,1,0:T(4,128)S(1)}, f32[8,4,128]{2,1,0:T(4,128)S(1)}, u32[]{:S(2)}, u32[]{:S(2)}) collective-permute-start(f32[8,4,128]{2,1,0:T(4,128)S(1)} %bitcast.89), channel_id=1, source_target_pairs={{0,192},{2,194},{4,196},{6,198},{8,200},{10,202},{12,204},{14,206}... | collective-permute-start | bytes 49160 | tf_op jit(solution)/shard_map/ppermute | solution.py:350
  98.5 4.8 %collective-permute-start.4 = (f32[8,4,128]{2,1,0:T(4,128)S(1)}, f32[8,4,128]{2,1,0:T(4,128)S(1)}, u32[]{:S(2)}, u32[]{:S(2)}) collective-permute-start(f32[8,4,128]{2,1,0:T(4,128)S(1)} %bitcast.86), channel_id=1, source_target_pairs={{0,128},{2,130},{4,132},{6,134},{8,136},{10,138},{12,140},{14,142}... | collective-permute-start | bytes 49160 | tf_op jit(solution)/shard_map/ppermute | solution.py:350
  98.7 4.8 %collective-permute-start.3 = (f32[8,4,128]{2,1,0:T(4,128)S(1)}, f32[8,4,128]{2,1,0:T(4,128)S(1)}, u32[]{:S(2)}, u32[]{:S(2)}) collective-permute-start(f32[8,4,128]{2,1,0:T(4,128)S(1)} %bitcast.83), channel_id=1, source_target_pairs={{0,64},{2,66},{4,68},{6,70},{8,72},{10,74},{12,76},{14,78},{16,80}... | collective-permute-start | bytes 49160 | tf_op jit(solution)/shard_map/ppermute | solution.py:350
  103.6 33.3 %collective-permute-start.6 = (f32[4,4,128]{2,0,1:T(4,128)S(1)}, f32[4,4,128]{2,0,1:T(4,128)S(1)}, u32[]{:S(2)}, u32[]{:S(2)}) collective-permute-start(f32[4,4,128]{2,0,1:T(4,128)S(1)} %get-tuple-element.38), channel_id=1, source_target_pairs={{0,8},{2,10},{4,12},{6,14},{8,16},{10,18},{12,20},{14,22},{16,24},... | collective-permute-start | bytes 24584 | tf_op jit(solution)/shard_map/ppermute | solution.py:350
  105.0 34.3 %collective-permute-start.7 = (f32[4,4,128]{2,0,1:T(4,128)S(1)}, f32[4,4,128]{2,0,1:T(4,128)S(1)}, u32[]{:S(2)}, u32[]{:S(2)}) collective-permute-start(f32[4,4,128]{2,0,1:T(4,128)S(1)} %get-tuple-element.37), channel_id=1, source_target_pairs={{0,16},{2,18},{4,20},{6,22},{8,24},{10,26},{12,28},{14,30},{16,32}... | collective-permute-start | bytes 24584 | tf_op jit(solution)/shard_map/ppermute | solution.py:350
  106.6 35.7 %collective-permute-start.8 = (f32[4,4,128]{2,0,1:T(4,128)S(1)}, f32[4,4,128]{2,0,1:T(4,128)S(1)}, u32[]{:S(2)}, u32[]{:S(2)}) collective-permute-start(f32[4,4,128]{2,0,1:T(4,128)S(1)} %get-tuple-element.36), channel_id=1, source_target_pairs={{0,24},{2,26},{4,28},{6,30},{8,32},{10,34},{12,36},{14,38},{16,40}... | collective-permute-start | bytes 24584 | tf_op jit(solution)/shard_map/ppermute | solution.py:350
  109.5 33.2 %collective-permute-start.9 = (f32[4,4,128]{2,0,1:T(4,128)S(1)}, f32[4,4,128]{2,0,1:T(4,128)S(1)}, u32[]{:S(2)}, u32[]{:S(2)}) collective-permute-start(f32[4,4,128]{2,0,1:T(4,128)S(1)} %get-tuple-element.35), channel_id=1, source_target_pairs={{0,32},{2,34},{4,36},{6,38},{8,40},{10,42},{12,44},{14,46},{16,48}... | collective-permute-start | bytes 24584 | tf_op jit(solution)/shard_map/ppermute | solution.py:350
  111.1 31.7 %collective-permute-start.10 = (f32[4,4,128]{2,0,1:T(4,128)S(1)}, f32[4,4,128]{2,0,1:T(4,128)S(1)}, u32[]{:S(2)}, u32[]{:S(2)}) collective-permute-start(f32[4,4,128]{2,0,1:T(4,128)S(1)} %get-tuple-element.34), channel_id=1, source_target_pairs={{0,40},{2,42},{4,44},{6,46},{8,48},{10,50},{12,52},{14,54},{16,56}... | collective-permute-start | bytes 24584 | tf_op jit(solution)/shard_map/ppermute | solution.py:350
  136.8 5.9 %collective-permute-start.11 = (f32[4,4,128]{2,0,1:T(4,128)S(1)}, f32[4,4,128]{2,0,1:T(4,128)S(1)}, u32[]{:S(2)}, u32[]{:S(2)}) collective-permute-start(f32[4,4,128]{2,0,1:T(4,128)S(1)} %get-tuple-element.33), channel_id=1, source_target_pairs={{0,48},{2,50},{4,52},{6,54},{8,56},{10,58},{12,60},{14,62},{16,0},... | collective-permute-start | bytes 24584 | tf_op jit(solution)/shard_map/ppermute | solution.py:350
  139.3 3.8 %collective-permute-start.12 = (f32[4,4,128]{2,0,1:T(4,128)S(1)}, f32[4,4,128]{2,0,1:T(4,128)S(1)}, u32[]{:S(2)}, u32[]{:S(2)}) collective-permute-start(f32[4,4,128]{2,0,1:T(4,128)S(1)} %get-tuple-element.32), channel_id=1, source_target_pairs={{0,56},{2,58},{4,60},{6,62},{8,0},{10,2},{12,4},{14,6},{16,8},{18,... | collective-permute-start | bytes 24584 | tf_op jit(solution)/shard_map/ppermute | solution.py:350
  143.2 4.1 %collective-permute-start.15 = (f32[4,8,128]{2,1,0:T(8,128)S(1)}, f32[4,8,128]{2,1,0:T(8,128)S(1)}, u32[]{:S(2)}, u32[]{:S(2)}) collective-permute-start(f32[4,8,128]{2,1,0:T(8,128)S(1)} %get-tuple-element.29), channel_id=1, source_target_pairs={{0,6},{2,0},{4,2},{6,4},{8,14},{10,8},{12,10},{14,12},{16,22},{18,... | collective-permute-start | bytes 49160 | tf_op jit(solution)/shard_map/ppermute | solution.py:350
  146.5 4.1 %collective-permute-start.14 = (f32[4,8,128]{2,1,0:T(8,128)S(1)}, f32[4,8,128]{2,1,0:T(8,128)S(1)}, u32[]{:S(2)}, u32[]{:S(2)}) collective-permute-start(f32[4,8,128]{2,1,0:T(8,128)S(1)} %get-tuple-element.30), channel_id=1, source_target_pairs={{0,4},{2,6},{4,0},{6,2},{8,12},{10,14},{12,8},{14,10},{16,20},{18,... | collective-permute-start | bytes 49160 | tf_op jit(solution)/shard_map/ppermute | solution.py:350
  146.5 4.1 %collective-permute-start.13 = (f32[4,8,128]{2,1,0:T(8,128)S(1)}, f32[4,8,128]{2,1,0:T(8,128)S(1)}, u32[]{:S(2)}, u32[]{:S(2)}) collective-permute-start(f32[4,8,128]{2,1,0:T(8,128)S(1)} %get-tuple-element.31), channel_id=1, source_target_pairs={{0,2},{2,4},{4,6},{6,0},{8,10},{10,12},{12,14},{14,8},{16,18},{18,... | collective-permute-start | bytes 49160 | tf_op jit(solution)/shard_map/ppermute | solution.py:350
  159.5 1.0 copy-start.4
  160.4 9.0 %copy-start.5 = (f32[32,64,128]{2,1,0:T(8,128)S(1)}, f32[32,64,128]{2,1,0:T(8,128)}, u32[]{:S(2)}) copy-start(f32[32,64,128]{2,1,0:T(8,128)} %copy-done.4) | copy-start | bytes 3145732
  160.4 9.0 %collective-permute-start.16 = (f32[32,64,128]{2,1,0:T(8,128)}, f32[32,64,128]{2,1,0:T(8,128)S(1)}, u32[]{:S(2)}, u32[]{:S(2)}) collective-permute-start(f32[32,64,128]{2,1,0:T(8,128)} %get-tuple-element.27), channel_id=1, source_target_pairs={{0,1},{1,0},{2,3},{3,2},{4,5},{5,4},{6,7},{7,6},{8,9},{9,8},{10,11... | collective-permute-start | bytes 3145736 | tf_op jit(solution)/shard_map/ppermute | solution.py:428
  169.2 2.4 %collective-permute-start.2 = (f32[24,64,128]{2,1,0:T(8,128)S(1)}, f32[24,64,128]{2,1,0:T(8,128)S(1)}, u32[]{:S(2)}, u32[]{:S(2)}) collective-permute-start(f32[24,64,128]{2,1,0:T(8,128)S(1)} %get-tuple-element.22), channel_id=1, source_target_pairs={{0,1},{1,0},{2,3},{3,2},{4,5},{5,4},{6,7},{7,6},{8,9},{9,8},{10,11... | collective-permute-start | bytes 2359304 | tf_op jit(solution)/shard_map/ppermute | solution.py:440
  169.4 2.2 %copy-start = (f32[6144,64]{0,1:T(8,128)S(1)}, f32[6144,64]{0,1:T(8,128)}, u32[]{:S(2)}) copy-start(f32[6144,64]{0,1:T(8,128)} %param.8) | copy-start | bytes 4718596

commit v3 on v2

--- a/solution.py
+++ b/solution.py
@@ -105,14 +105,13 @@
     lax.fori_loop(0, peers, row, 0, unroll=8)
 
 
-def coords(chip):
-    n0, n1, n2 = GRID
-    return lax.div(chip, n1 * n2), lax.rem(lax.div(chip, n2), n1), lax.rem(chip, n2)
-
-
 def combine(chip, other, sign):
-    x, y, z = (lax.rem(a + sign * b + n, n) for a, b, n in zip(coords(chip), coords(other), GRID))
-    return (x * GRID[1] + y) * GRID[2] + z
+    result, shift = 0, 0
+    for n in reversed(GRID):
+        mask = (n - 1) << shift
+        result = result | (((chip & mask) + sign * (other & mask)) & mask)
+        shift += n.bit_length() - 1
+    return result
 
 
 def ident_kernel(core_ref, own_ref, peer_ref, count_ref, idt_ref, id_ref, weight_ref):
@@ -131,7 +130,7 @@
     weight_ref[...] = count_weight(count_ref[...])
 
 
-GROUP = 16
+GROUP = 48
 
 
 def score_kernel(
@@ -265,20 +264,30 @@
         out_ref[:, n * blk : (n + 1) * blk] = old - STEP * (grad + DECAY * old)
 
 
-def collect_kernel(core_ref, list_ref, back_ref, count_ref, keep_ref, send_ref, grad, weights):
+def collect_kernel(core_ref, list_ref, back_hbm, count_ref, keep_ref, send_ref, grad, weights, back_ref, sems):
     core = core_ref[0]
     pairs, half_cols, blk = keep_ref.shape
     half = blk // 2
+    parts = sems.shape[0]
+    count = back_ref.shape[0] // parts
+
+    def take(p):
+        at = pl.ds(p * count, count)
+        return pltpu.make_async_copy(back_hbm.at[at], back_ref.at[at], sems.at[p])
+
+    for p in range(parts):
+        take(p).start()
     grad[...] = jnp.zeros_like(grad)
     weight = count_weight(count_ref[...]).astype(BF16).astype(F32)
     weights[...] = jnp.where(core == 0, weight, pltpu.roll(weight, half, 1))
 
     def add(e, _):
-        r = list_ref[e]
-        grad[r] += back_ref[e].astype(F32)
-        return 0
-
-    lax.fori_loop(0, back_ref.shape[0], add, 0, unroll=8)
+        grad[list_ref[e]] += back_ref[e].astype(F32)
+        return 0
+
+    for p in range(parts):
+        take(p).wait()
+        lax.fori_loop(p * count, (p + 1) * count, add, 0, unroll=8)
     low = low_lanes(half)
 
     def pair(m, _):
@@ -290,15 +299,17 @@
         send_ref[m] = jnp.where(core == 0, last, first)
         return 0
 
-    lax.fori_loop(0, pairs, pair, 0, unroll=2)
-
-
-def record_update_kernel(core_ref, rec_ref, keep_ref, recv_ref, out_ref):
+    lax.fori_loop(0, pairs, pair, 0, unroll=4)
+
+
+def record_update_kernel(core_ref, rec_ref, keep_ref, recv_ref, out_hbm, out_ref, sems):
     core = core_ref[0]
     pairs, _, blk = keep_ref.shape
     low = low_lanes(blk // 2)
-
-    def pair(m, _):
+    parts = sems.shape[0]
+    width = out_ref.shape[1] // parts
+    copies = []
+    for m in range(pairs):
         keep, recv = keep_ref[m], recv_ref[m]
         half0 = jnp.where(core == 0, keep, recv)
         half1 = jnp.where(core == 0, recv, keep)
@@ -307,12 +318,16 @@
             jnp.where(low, pltpu.roll(half0, blk // 2, 1), half1),
         )
         for k, grad in enumerate(grads):
-            at = pl.ds(pl.multiple_of(m * 2 * blk + k * blk, blk), blk)
+            at = slice((2 * m + k) * blk, (2 * m + k + 1) * blk)
             old = rec_ref[:, at]
             out_ref[:, at] = old - STEP * (grad + DECAY * old)
-        return 0
-
-    lax.fori_loop(0, pairs, pair, 0, unroll=2)
+        if (m + 1) % (pairs // parts) == 0:
+            p = len(copies)
+            at = pl.ds(p * width, width)
+            copies.append(pltpu.make_async_copy(out_ref.at[:, at], out_hbm.at[:, at], sems.at[p]))
+            copies[-1].start()
+    for copy in copies:
+        copy.wait()
 
 
 def call(kernel, outs, ins, scratch=(), sems=(), name=None):
@@ -335,7 +350,8 @@
     width = rows.shape[1]
     chips = GRID[0] * GRID[1] * GRID[2]
     rows = rows.reshape(*GRID, width)
-    for axis, extent in enumerate(GRID):
+    for axis in (0, 2, 1):
+        extent = GRID[axis]
         stride = 1
         for n in GRID[axis + 1 :]:
             stride *= n
@@ -382,8 +398,13 @@
         [((recs, half, rank), BF16), (chunk_shape, BF16)],
         [4],
         name="pack",
-    )(core, sends, keep, recv)
+    )(core, in_hbm(sends), keep, recv)
+    late_count, chunks = lax.optimization_barrier((rec_count, chunks))
     arrived = exchange(chunks)
+    (weights,) = call(
+        weigh_kernel, [((peers, blk), F32)], [SMEM, SMEM, SMEM, VMEM], [((recs, blk), F32)], name="weigh"
+    )(core, chip, sends, late_count)
+    arrived_weight = by_offsets(weights)
 
     (id_half,) = call(cast_kernel, [((ids, half_cols, blk), BF16)], [VMEM], name="cast")(id_t)
     id_peer = swap(id_half)
@@ -393,6 +414,7 @@
         [SMEM, VMEM, VMEM, VMEM],
         name="ident",
     )(core, id_half, id_peer, id_count)
+    arrived_weight, id_weight = lax.optimization_barrier((arrived_weight, id_weight))
     resid_shape = (blocks, half, blk)
     groups = blocks // GROUP
     resid, slot_grad = call(
@@ -412,11 +434,6 @@
     )(core, slot_of_block, id_of_block, arrived, id_weight, in_hbm(idt), in_hbm(id_rows), in_hbm(observed))
     returned = exchange(slot_grad)
 
-    (weights,) = call(
-        weigh_kernel, [((peers, blk), F32)], [SMEM, SMEM, SMEM, VMEM], [((recs, blk), F32)], name="weigh"
-    )(core, chip, sends, rec_count)
-    weights, resid = lax.optimization_barrier((weights, resid))
-    arrived_weight = by_offsets(weights)
     id_keep, id_send = call(
         ident_grad_kernel,
         [((ids, half_cols, blk), F32)] * 2,
@@ -433,14 +450,20 @@
     rec_keep, rec_send = call(
         collect_kernel,
         [(half_shape, F32), (half_shape, F32)],
-        [SMEM, SMEM, VMEM, VMEM],
-        [((recs, half, rank), F32), ((recs, blk), F32)],
+        [SMEM, SMEM, HBM, VMEM],
+        [((recs, half, rank), F32), ((recs, blk), F32), (chunk_shape, BF16)],
+        [8],
         name="collect",
-    )(core, sends, returned, rec_count)
+    )(core, sends, in_hbm(returned), rec_count)
     rec_recv = swap(rec_send)
-    (new_rec_t,) = call(record_update_kernel, [(rec_t.shape, F32)], [SMEM, VMEM, VMEM, VMEM], name="record_update")(
-        core, rec_t, rec_keep, rec_recv
-    )
+    (new_rec_t,) = call(
+        record_update_kernel,
+        [(rec_t.shape, F32, True)],
+        [SMEM, VMEM, VMEM, VMEM],
+        [(rec_t.shape, F32)],
+        [4],
+        name="record_update",
+    )(core, rec_t, rec_keep, rec_recv)
     return new_rec_t.T, new_id_t.T
 
 

time: 174 us -> 171 us (0.983)
  starting transfers between devices: 56.4 us -> 73.3 us
  waiting for transfers between devices: 78.7 us -> 64.2 us
  Pallas kernels: 34.2 us -> 28.8 us
    all_to_all x1, waiting for transfers between devices: 43.4 us -> 0.01 us  [body(): arrived = exchange(chunks)]
    all_to_all x1, waiting for transfers between devices: 0.01 us -> 31.5 us  [body(): returned = exchange(slot_grad)]
    ppermute x1, starting transfers between devices: 0.18 us -> 7.9 us  [body(): rec_recv = swap(rec_send)]
    all_to_all x1, starting transfers between devices: 10.5 us -> 13.9 us  [body(): returned = exchange(slot_grad)]
    ppermute x1, starting transfers between devices: 0.74 us -> 4.03 us  [body(): id_peer = swap(id_half)]
    ppermute x13, starting transfers between devices: 22.8 us -> 25.4 us  [by_offsets(): part = lax.ppermute(part, 'gx', pairs)]
    unnamed x24 -> x29, local copies, waits for them, and re-layouts: 3.6 us -> 2.99 us
  transfers between devices with their start and end apart: 19 -> 19, of which waited for: 12 -> 9; matrix products, arithmetic and copies ran while one was open for 0% -> 0% of each run, Pallas kernels for 10% -> 9%
where the time goes in v3:
time: 171 us
  starting transfers between devices  73.3 us (43%)
  waiting for transfers between devices  64.2 us (38%)
  Pallas kernels  28.8 us (17%)
  local copies, waits for them, and re-layouts  3.05 us (2%)
    all_to_all x1, waiting for transfers between devices, body(): returned = exchange(slot_grad)  31.5 us
    ppermute x13, waiting for transfers between devices, by_offsets(): part = lax.ppermute(part, 'gx', pairs)  30.7 us
    ppermute x13, starting transfers between devices, by_offsets(): part = lax.ppermute(part, 'gx', pairs)  25.4 us
    all_to_all x1, starting transfers between devices, body(): returned = exchange(slot_grad)  13.9 us
    all_to_all x1, starting transfers between devices, body(): arrived = exchange(chunks)  13.9 us
    pallas_call x1, Pallas kernels, body(): call(score_kernel, [(resid_shape, BF16, True), (chunk_shape, BF16, True)]...  8.28 us
    ppermute x1, starting transfers between devices, body(): rec_recv = swap(rec_send)  7.9 us
    pallas_call x1, Pallas kernels, body(): call(ident_grad_kernel, [((ids, half_cols, blk), F32)] * 2, [SMEM] * 4 +...  7.58 us
  transfers between devices with their start and end apart: 19, of which 9 were waited for; matrix products, arithmetic and copies ran while one was open for 0% of the time, Pallas kernels for 9%

profile of v3, /device:TPU:1, one launch (start us, length us, event | category | flops | bytes accessed | tf_op | source)
XLA Modules:
  0.0 170.6 jit_solution(1148919653650187850)
XLA Ops:
  0.6 1.5 split.1
  2.2 3.3 %collective-permute-start = (bf16[24,64,128]{2,1,0:T(8,128)(2,1)S(1)}, bf16[24,64,128]{2,1,0:T(8,128)(2,1)S(1)}, u32[]{:S(2)}, u32[]{:S(2)}) collective-permute-start(bf16[24,64,128]{2,1,0:T(8,128)(2,1)S(1)} %get-tuple-element.18), channel_id=1, source_target_pairs={{0,1},{1,0},{2,3},{3,2},{4,5},{5,4},{6,7},{7,6},{8,9},{9,8},{10,11... | collective-permute-start | bytes 1179656 | tf_op jit(solution)/shard_map/ppermute | solution.py:393
  5.5 1.3 collective-permute-done.recv_ref
  6.9 2.8 %pack.1 = bf16[128,64,128]{2,1,0:T(8,128)(2,1)} custom-call(s32[1]{0:T(128)} %bitcast.core_ref, s32[128]{0:T(128)} %bitcast.83, bf16[24,64,128]{2,1,0:T(8,128)(2,1)S(1)} %get-tuple-element.17.keep_ref, bf16[24,64,128]{2,1,0:T(8,128)(2,1)S(1)} %collective-permute-done.recv_ref), custom_call_target="tpu_custom_call" | custom-call | tf_op jit(solution)/shard_map/pack/pallas_call | solution.py:394
  9.6 0.0 copy-start.6
  9.6 0.0 copy-start.8
  9.6 0.0 copy-start.1
  9.7 13.9 %all-to-all-start = ((bf16[128,64,128]{2,1,0:T(8,128)(2,1)}), bf16[128,64,128]{2,1,0:T(8,128)(2,1)S(1)}, u32[]{:S(2)}, u32[]{:S(2)}) async-start(bf16[128,64,128]{2,1,0:T(8,128)(2,1)} %pack.1), calls=%async_computation | async-start | bytes 4194304 | tf_op jit(solution)/shard_map/all_to_all | solution.py:403
  23.6 0.0 copy-start.9
  23.6 0.0 copy-start.10
  23.6 1.2 weigh.1
  24.9 0.8 collective-permute-start.1
  25.6 2.8 %collective-permute-start.2 = (f32[8,4,128]{2,0,1:T(8,128)S(1)}, f32[8,4,128]{2,0,1:T(8,128)S(1)}, u32[]{:S(2)}, u32[]{:S(2)}) collective-permute-start(f32[8,4,128]{2,0,1:T(8,128)S(1)} %copy.11), channel_id=1, source_target_pairs={{0,128},{2,130},{4,132},{6,134},{8,136},{10,138},{12,140},{14,142}... | collective-permute-start | bytes 49160 | tf_op jit(solution)/shard_map/ppermute | solution.py:366
  28.5 1.0 collective-permute-start.3
  29.4 1.4 collective-permute-done.1
  30.8 0.6 collective-permute-done.3
  31.5 0.1 pad_maximum_fusion
  31.6 2.4 %collective-permute-start.6 = (f32[4,8,128]{2,0,1:T(4,128)S(1)}, f32[4,8,128]{2,0,1:T(4,128)S(1)}, u32[]{:S(2)}, u32[]{:S(2)}) collective-permute-start(f32[4,8,128]{2,0,1:T(4,128)S(1)} %get-tuple-element.40), channel_id=1, source_target_pairs={{0,6},{2,0},{4,2},{6,4},{8,14},{10,8},{12,10},{14,12},{16,22},{18,... | collective-permute-start | bytes 49160 | tf_op jit(solution)/shard_map/ppermute | solution.py:366
  33.9 0.6 collective-permute-start.5
  34.5 0.5 collective-permute-start.4
  35.1 0.1 cast.1.own_ref
  35.1 4.0 %collective-permute-start.14 = (bf16[32,64,128]{2,1,0:T(8,128)(2,1)S(1)}, bf16[32,64,128]{2,1,0:T(8,128)(2,1)S(1)}, u32[]{:S(2)}, u32[]{:S(2)}) collective-permute-start(bf16[32,64,128]{2,1,0:T(8,128)(2,1)S(1)} %cast.1.own_ref), channel_id=1, source_target_pairs={{0,1},{1,0},{2,3},{3,2},{4,5},{5,4},{6,7},{7,6},{8,9},{9,8},{10,11... | collective-permute-start | bytes 1572872 | tf_op jit(solution)/shard_map/ppermute | solution.py:410
  39.2 0.1 pad_maximum_fusion.1
  39.3 0.9 collective-permute-start.7
  40.2 1.8 %collective-permute-start.13 = (f32[4,4,128]{2,1,0:T(4,128)S(1)}, f32[4,4,128]{2,1,0:T(4,128)S(1)}, u32[]{:S(2)}, u32[]{:S(2)}) collective-permute-start(f32[4,4,128]{2,1,0:T(4,128)S(1)} %get-tuple-element.32), channel_id=1, source_target_pairs={{0,56},{2,58},{4,60},{6,62},{8,0},{10,2},{12,4},{14,6},{16,8},{18,... | collective-permute-start | bytes 24584 | tf_op jit(solution)/shard_map/ppermute | solution.py:366
  42.0 2.2 %collective-permute-start.12 = (f32[4,4,128]{2,1,0:T(4,128)S(1)}, f32[4,4,128]{2,1,0:T(4,128)S(1)}, u32[]{:S(2)}, u32[]{:S(2)}) collective-permute-start(f32[4,4,128]{2,1,0:T(4,128)S(1)} %get-tuple-element.33), channel_id=1, source_target_pairs={{0,48},{2,50},{4,52},{6,54},{8,56},{10,58},{12,60},{14,62},{16,0},... | collective-permute-start | bytes 24584 | tf_op jit(solution)/shard_map/ppermute | solution.py:366
  44.3 3.2 %collective-permute-start.11 = (f32[4,4,128]{2,1,0:T(4,128)S(1)}, f32[4,4,128]{2,1,0:T(4,128)S(1)}, u32[]{:S(2)}, u32[]{:S(2)}) collective-permute-start(f32[4,4,128]{2,1,0:T(4,128)S(1)} %get-tuple-element.34), channel_id=1, source_target_pairs={{0,40},{2,42},{4,44},{6,46},{8,48},{10,50},{12,52},{14,54},{16,56}... | collective-permute-start | bytes 24584 | tf_op jit(solution)/shard_map/ppermute | solution.py:366
  47.5 20.0 %collective-permute-done.7 = f32[4,4,128]{2,1,0:T(4,128)S(1)} collective-permute-done((f32[4,4,128]{2,1,0:T(4,128)S(1)}, f32[4,4,128]{2,1,0:T(4,128)S(1)}, u32[]{:S(2)}, u32[]{:S(2)}) %collective-permute-start.7) | collective-permute-done | bytes 8224 | tf_op jit(solution)/shard_map/ppermute | solution.py:366
  67.5 1.8 %collective-permute-start.8 = (f32[4,4,128]{2,1,0:T(4,128)S(1)}, f32[4,4,128]{2,1,0:T(4,128)S(1)}, u32[]{:S(2)}, u32[]{:S(2)}) collective-permute-start(f32[4,4,128]{2,1,0:T(4,128)S(1)} %get-tuple-element.37), channel_id=1, source_target_pairs={{0,16},{2,18},{4,20},{6,22},{8,24},{10,26},{12,28},{14,30},{16,32}... | collective-permute-start | bytes 24584 | tf_op jit(solution)/shard_map/ppermute | solution.py:366
  69.3 3.1 %collective-permute-done.8 = f32[4,4,128]{2,1,0:T(4,128)S(1)} collective-permute-done((f32[4,4,128]{2,1,0:T(4,128)S(1)}, f32[4,4,128]{2,1,0:T(4,128)S(1)}, u32[]{:S(2)}, u32[]{:S(2)}) %collective-permute-start.8) | collective-permute-done | bytes 8224 | tf_op jit(solution)/shard_map/ppermute | solution.py:366
  72.4 2.7 %collective-permute-start.9 = (f32[4,4,128]{2,1,0:T(4,128)S(1)}, f32[4,4,128]{2,1,0:T(4,128)S(1)}, u32[]{:S(2)}, u32[]{:S(2)}) collective-permute-start(f32[4,4,128]{2,1,0:T(4,128)S(1)} %get-tuple-element.36), channel_id=1, source_target_pairs={{0,24},{2,26},{4,28},{6,30},{8,32},{10,34},{12,36},{14,38},{16,40}... | collective-permute-start | bytes 24584 | tf_op jit(solution)/shard_map/ppermute | solution.py:366
  75.1 3.7 %collective-permute-done.9 = f32[4,4,128]{2,1,0:T(4,128)S(1)} collective-permute-done((f32[4,4,128]{2,1,0:T(4,128)S(1)}, f32[4,4,128]{2,1,0:T(4,128)S(1)}, u32[]{:S(2)}, u32[]{:S(2)}) %collective-permute-start.9) | collective-permute-done | bytes 8224 | tf_op jit(solution)/shard_map/ppermute | solution.py:366
  78.8 4.6 %collective-permute-start.10 = (f32[4,4,128]{2,1,0:T(4,128)S(1)}, f32[4,4,128]{2,1,0:T(4,128)S(1)}, u32[]{:S(2)}, u32[]{:S(2)}) collective-permute-start(f32[4,4,128]{2,1,0:T(4,128)S(1)} %get-tuple-element.35), channel_id=1, source_target_pairs={{0,32},{2,34},{4,36},{6,38},{8,40},{10,42},{12,44},{14,46},{16,48}... | collective-permute-start | bytes 24584 | tf_op jit(solution)/shard_map/ppermute | solution.py:366
  83.5 1.8 %collective-permute-done.10 = f32[4,4,128]{2,1,0:T(4,128)S(1)} collective-permute-done((f32[4,4,128]{2,1,0:T(4,128)S(1)}, f32[4,4,128]{2,1,0:T(4,128)S(1)}, u32[]{:S(2)}, u32[]{:S(2)}) %collective-permute-start.10) | collective-permute-done | bytes 8224 | tf_op jit(solution)/shard_map/ppermute | solution.py:366
  85.3 1.7 ident.1
  87.1 1.0 copy-done.2
  88.0 1.0 copy-done.3
  89.0 8.3 %score.1 = (bf16[192,64,128]{2,1,0:T(8,128)(2,1)}, bf16[128,64,128]{2,1,0:T(8,128)(2,1)}) custom-call(s32[1]{0:T(128)} %bitcast.core_ref, s32[192]{0:T(256)S(1)} %copy-done.9, s32[192]{0:T(256)S(1)} %copy-done.10, bf16[128,64,128]{2,1,0:T(8,128)(2,1)S(1)} %all-to-all-done.rows_ref, f32[32,128]{1,0:T(8,128)S(1)} %get-tuple-element.22.weight_ref, ...), custom_call_target="tpu_custom_call" | custom-call | tf_op jit(solution)/shard_map/score/pallas_call | solution.py:420
  97.3 13.9 %all-to-all-start.1 = ((bf16[128,64,128]{2,1,0:T(8,128)(2,1)}), bf16[128,64,128]{2,1,0:T(8,128)(2,1)}, u32[]{:S(2)}, u32[]{:S(2)}) async-start(bf16[128,64,128]{2,1,0:T(8,128)(2,1)} %get-tuple-element.25), calls=%async_computation.1 | async-start | bytes 4194304 | tf_op jit(solution)/shard_map/all_to_all | solution.py:435
  111.2 7.6 %ident_grad.1 = (f32[32,64,128]{2,1,0:T(8,128)S(1)}, f32[32,64,128]{2,1,0:T(8,128)}) custom-call(s32[1]{0:T(128)} %bitcast.core_ref, s32[1]{0:T(128)} %bitcast.4.chip_ref, s32[192]{0:T(256)S(1)} %copy-done.9, s32[192]{0:T(256)S(1)} %copy-done.10, bf16[128,64,128]{2,1,0:T(8,128)(2,1)S(1)} %all-to-all-done.rows_ref, f32[128,128]{1,0:T(8,128)S(1)} %bitcast.81, ...), custom_call_target="tpu_custom_call" | custom-call | tf_op jit(solution)/shard_map/ident_grad/pallas_call | solution.py:437
  118.8 1.0 copy-done.4
  119.8 4.8 %collective-permute-start.16 = (f32[32,64,128]{2,1,0:T(8,128)}, f32[32,64,128]{2,1,0:T(8,128)S(1)}, u32[]{:S(2)}, u32[]{:S(2)}) collective-permute-start(f32[32,64,128]{2,1,0:T(8,128)} %get-tuple-element.31), channel_id=1, source_target_pairs={{0,1},{1,0},{2,3},{3,2},{4,5},{5,4},{6,7},{7,6},{8,9},{9,8},{10,11... | collective-permute-start | bytes 3145736 | tf_op jit(solution)/shard_map/ppermute | solution.py:445
  124.6 31.5 %all-to-all-done.1.back_hbm = bf16[128,64,128]{2,1,0:T(8,128)(2,1)} async-done(((bf16[128,64,128]{2,1,0:T(8,128)(2,1)}), bf16[128,64,128]{2,1,0:T(8,128)(2,1)}, u32[]{:S(2)}, u32[]{:S(2)}) %all-to-all-start.1) | async-done | bytes 2097184 | tf_op jit(solution)/shard_map/all_to_all | solution.py:435
  156.1 3.1 %collect.1 = (f32[24,64,128]{2,1,0:T(8,128)S(1)}, f32[24,64,128]{2,1,0:T(8,128)S(1)}) custom-call(s32[1]{0:T(128)} %bitcast.core_ref, s32[128]{0:T(128)S(1)} %bitcast.85, bf16[128,64,128]{2,1,0:T(8,128)(2,1)} %all-to-all-done.1.back_hbm, s32[48,128]{1,0:T(8,128)S(1)} %bitcast.80), custom_call_target="tpu_custom_call" | custom-call | tf_op jit(solution)/shard_map/collect/pallas_call | solution.py:450
  159.2 7.9 %collective-permute-start.15 = (f32[24,64,128]{2,1,0:T(8,128)S(1)}, f32[24,64,128]{2,1,0:T(8,128)S(1)}, u32[]{:S(2)}, u32[]{:S(2)}) collective-permute-start(f32[24,64,128]{2,1,0:T(8,128)S(1)} %get-tuple-element.27), channel_id=1, source_target_pairs={{0,1},{1,0},{2,3},{3,2},{4,5},{5,4},{6,7},{7,6},{8,9},{9,8},{10,11... | collective-permute-start | bytes 2359304 | tf_op jit(solution)/shard_map/ppermute | solution.py:458
  167.1 1.2 ident_update.1
  168.3 0.7 collective-permute-done.15.recv_ref
  169.0 1.4 record_update.1
  (39 shorter events, 0.2 us)
Async XLA Ops:
  2.2 4.7 %collective-permute-start = (bf16[24,64,128]{2,1,0:T(8,128)(2,1)S(1)}, bf16[24,64,128]{2,1,0:T(8,128)(2,1)S(1)}, u32[]{:S(2)}, u32[]{:S(2)}) collective-permute-start(bf16[24,64,128]{2,1,0:T(8,128)(2,1)S(1)} %get-tuple-element.18), channel_id=1, source_target_pairs={{0,1},{1,0},{2,3},{3,2},{4,5},{5,4},{6,7},{7,6},{8,9},{9,8},{10,11... | collective-permute-start | bytes 1179656 | tf_op jit(solution)/shard_map/ppermute | solution.py:393
  9.6 14.0 %copy-start.6 = (s32[6144]{0:T(1024)S(1)}, s32[6144]{0:T(1024)}, u32[]{:S(2)}) copy-start(s32[6144]{0:T(1024)} %param.10) | copy-start | bytes 73732
  9.6 14.0 %copy-start.8 = (s32[128,1]{0,1:T(1,128)S(1)}, s32[128,1]{0,1:T(1,128)}, u32[]{:S(2)}) copy-start(s32[128,1]{0,1:T(1,128)} %param.13) | copy-start | bytes 1540
  9.6 25.4 %copy-start.1 = (f32[4096,64]{0,1:T(8,128)S(1)}, f32[4096,64]{0,1:T(8,128)}, u32[]{:S(2)}) copy-start(f32[4096,64]{0,1:T(8,128)} %param.9) | copy-start | bytes 3145732
  9.7 79.3 %all-to-all-start = ((bf16[128,64,128]{2,1,0:T(8,128)(2,1)}), bf16[128,64,128]{2,1,0:T(8,128)(2,1)S(1)}, u32[]{:S(2)}, u32[]{:S(2)}) async-start(bf16[128,64,128]{2,1,0:T(8,128)(2,1)} %pack.1), calls=%async_computation | async-start | bytes 4194304 | tf_op jit(solution)/shard_map/all_to_all | solution.py:403
  23.6 61.8 %copy-start.7 = (s32[4096]{0:T(1024)S(1)}, s32[4096]{0:T(1024)}, u32[]{:S(2)}) copy-start(s32[4096]{0:T(1024)} %param.11) | copy-start | bytes 49156
  23.6 65.4 %copy-start.9 = (s32[192]{0:T(256)S(1)}, s32[192]{0:T(256)}, u32[]{:S(2)}) copy-start(s32[192]{0:T(256)} %slot_ref.3) | copy-start | bytes 2308
  23.6 65.4 %copy-start.10 = (s32[192]{0:T(256)S(1)}, s32[192]{0:T(256)}, u32[]{:S(2)}) copy-start(s32[192]{0:T(256)} %ident_ref.3) | copy-start | bytes 2308
  24.9 6.0 %collective-permute-start.1 = (f32[8,4,128]{2,0,1:T(8,128)S(1)}, f32[8,4,128]{2,0,1:T(8,128)S(1)}, u32[]{:S(2)}, u32[]{:S(2)}) collective-permute-start(f32[8,4,128]{2,0,1:T(8,128)S(1)} %copy.10), channel_id=1, source_target_pairs={{0,64},{2,66},{4,68},{6,70},{8,72},{10,74},{12,76},{14,78},{16,80}... | collective-permute-start | bytes 49160 | tf_op jit(solution)/shard_map/ppermute | solution.py:366
  25.6 5.2 %collective-permute-start.2 = (f32[8,4,128]{2,0,1:T(8,128)S(1)}, f32[8,4,128]{2,0,1:T(8,128)S(1)}, u32[]{:S(2)}, u32[]{:S(2)}) collective-permute-start(f32[8,4,128]{2,0,1:T(8,128)S(1)} %copy.11), channel_id=1, source_target_pairs={{0,128},{2,130},{4,132},{6,134},{8,136},{10,138},{12,140},{14,142}... | collective-permute-start | bytes 49160 | tf_op jit(solution)/shard_map/ppermute | solution.py:366
  28.5 3.0 %collective-permute-start.3 = (f32[8,4,128]{2,0,1:T(8,128)S(1)}, f32[8,4,128]{2,0,1:T(8,128)S(1)}, u32[]{:S(2)}, u32[]{:S(2)}) collective-permute-start(f32[8,4,128]{2,0,1:T(8,128)S(1)} %copy.12), channel_id=1, source_target_pairs={{0,192},{2,194},{4,196},{6,198},{8,200},{10,202},{12,204},{14,206}... | collective-permute-start | bytes 49160 | tf_op jit(solution)/shard_map/ppermute | solution.py:366
  31.6 7.6 %collective-permute-start.6 = (f32[4,8,128]{2,0,1:T(4,128)S(1)}, f32[4,8,128]{2,0,1:T(4,128)S(1)}, u32[]{:S(2)}, u32[]{:S(2)}) collective-permute-start(f32[4,8,128]{2,0,1:T(4,128)S(1)} %get-tuple-element.40), channel_id=1, source_target_pairs={{0,6},{2,0},{4,2},{6,4},{8,14},{10,8},{12,10},{14,12},{16,22},{18,... | collective-permute-start | bytes 49160 | tf_op jit(solution)/shard_map/ppermute | solution.py:366
  33.9 5.2 %collective-permute-start.5 = (f32[4,8,128]{2,0,1:T(4,128)S(1)}, f32[4,8,128]{2,0,1:T(4,128)S(1)}, u32[]{:S(2)}, u32[]{:S(2)}) collective-permute-start(f32[4,8,128]{2,0,1:T(4,128)S(1)} %get-tuple-element.41), channel_id=1, source_target_pairs={{0,4},{2,6},{4,0},{6,2},{8,12},{10,14},{12,8},{14,10},{16,20},{18,... | collective-permute-start | bytes 49160 | tf_op jit(solution)/shard_map/ppermute | solution.py:366
  34.5 4.6 %collective-permute-start.4 = (f32[4,8,128]{2,0,1:T(4,128)S(1)}, f32[4,8,128]{2,0,1:T(4,128)S(1)}, u32[]{:S(2)}, u32[]{:S(2)}) collective-permute-start(f32[4,8,128]{2,0,1:T(4,128)S(1)} %get-tuple-element.42), channel_id=1, source_target_pairs={{0,2},{2,4},{4,6},{6,0},{8,10},{10,12},{12,14},{14,8},{16,18},{18,... | collective-permute-start | bytes 49160 | tf_op jit(solution)/shard_map/ppermute | solution.py:366
  35.1 50.2 %collective-permute-start.14 = (bf16[32,64,128]{2,1,0:T(8,128)(2,1)S(1)}, bf16[32,64,128]{2,1,0:T(8,128)(2,1)S(1)}, u32[]{:S(2)}, u32[]{:S(2)}) collective-permute-start(bf16[32,64,128]{2,1,0:T(8,128)(2,1)S(1)} %cast.1.own_ref), channel_id=1, source_target_pairs={{0,1},{1,0},{2,3},{3,2},{4,5},{5,4},{6,7},{7,6},{8,9},{9,8},{10,11... | collective-permute-start | bytes 1572872 | tf_op jit(solution)/shard_map/ppermute | solution.py:410
  39.3 28.3 %collective-permute-start.7 = (f32[4,4,128]{2,1,0:T(4,128)S(1)}, f32[4,4,128]{2,1,0:T(4,128)S(1)}, u32[]{:S(2)}, u32[]{:S(2)}) collective-permute-start(f32[4,4,128]{2,1,0:T(4,128)S(1)} %get-tuple-element.38), channel_id=1, source_target_pairs={{0,8},{2,10},{4,12},{6,14},{8,16},{10,18},{12,20},{14,22},{16,24},... | collective-permute-start | bytes 24584 | tf_op jit(solution)/shard_map/ppermute | solution.py:366
  40.2 45.1 %collective-permute-start.13 = (f32[4,4,128]{2,1,0:T(4,128)S(1)}, f32[4,4,128]{2,1,0:T(4,128)S(1)}, u32[]{:S(2)}, u32[]{:S(2)}) collective-permute-start(f32[4,4,128]{2,1,0:T(4,128)S(1)} %get-tuple-element.32), channel_id=1, source_target_pairs={{0,56},{2,58},{4,60},{6,62},{8,0},{10,2},{12,4},{14,6},{16,8},{18,... | collective-permute-start | bytes 24584 | tf_op jit(solution)/shard_map/ppermute | solution.py:366
  42.0 43.3 %collective-permute-start.12 = (f32[4,4,128]{2,1,0:T(4,128)S(1)}, f32[4,4,128]{2,1,0:T(4,128)S(1)}, u32[]{:S(2)}, u32[]{:S(2)}) collective-permute-start(f32[4,4,128]{2,1,0:T(4,128)S(1)} %get-tuple-element.33), channel_id=1, source_target_pairs={{0,48},{2,50},{4,52},{6,54},{8,56},{10,58},{12,60},{14,62},{16,0},... | collective-permute-start | bytes 24584 | tf_op jit(solution)/shard_map/ppermute | solution.py:366
  44.3 41.0 %collective-permute-start.11 = (f32[4,4,128]{2,1,0:T(4,128)S(1)}, f32[4,4,128]{2,1,0:T(4,128)S(1)}, u32[]{:S(2)}, u32[]{:S(2)}) collective-permute-start(f32[4,4,128]{2,1,0:T(4,128)S(1)} %get-tuple-element.34), channel_id=1, source_target_pairs={{0,40},{2,42},{4,44},{6,46},{8,48},{10,50},{12,52},{14,54},{16,56}... | collective-permute-start | bytes 24584 | tf_op jit(solution)/shard_map/ppermute | solution.py:366
  67.5 4.9 %collective-permute-start.8 = (f32[4,4,128]{2,1,0:T(4,128)S(1)}, f32[4,4,128]{2,1,0:T(4,128)S(1)}, u32[]{:S(2)}, u32[]{:S(2)}) collective-permute-start(f32[4,4,128]{2,1,0:T(4,128)S(1)} %get-tuple-element.37), channel_id=1, source_target_pairs={{0,16},{2,18},{4,20},{6,22},{8,24},{10,26},{12,28},{14,30},{16,32}... | collective-permute-start | bytes 24584 | tf_op jit(solution)/shard_map/ppermute | solution.py:366
  72.4 6.4 %collective-permute-start.9 = (f32[4,4,128]{2,1,0:T(4,128)S(1)}, f32[4,4,128]{2,1,0:T(4,128)S(1)}, u32[]{:S(2)}, u32[]{:S(2)}) collective-permute-start(f32[4,4,128]{2,1,0:T(4,128)S(1)} %get-tuple-element.36), channel_id=1, source_target_pairs={{0,24},{2,26},{4,28},{6,30},{8,32},{10,34},{12,36},{14,38},{16,40}... | collective-permute-start | bytes 24584 | tf_op jit(solution)/shard_map/ppermute | solution.py:366
  78.8 6.4 %collective-permute-start.10 = (f32[4,4,128]{2,1,0:T(4,128)S(1)}, f32[4,4,128]{2,1,0:T(4,128)S(1)}, u32[]{:S(2)}, u32[]{:S(2)}) collective-permute-start(f32[4,4,128]{2,1,0:T(4,128)S(1)} %get-tuple-element.35), channel_id=1, source_target_pairs={{0,32},{2,34},{4,36},{6,38},{8,40},{10,42},{12,44},{14,46},{16,48}... | collective-permute-start | bytes 24584 | tf_op jit(solution)/shard_map/ppermute | solution.py:366
  87.0 1.0 copy-start.2
  88.0 1.0 copy-start.3
  97.3 58.8 %all-to-all-start.1 = ((bf16[128,64,128]{2,1,0:T(8,128)(2,1)}), bf16[128,64,128]{2,1,0:T(8,128)(2,1)}, u32[]{:S(2)}, u32[]{:S(2)}) async-start(bf16[128,64,128]{2,1,0:T(8,128)(2,1)} %get-tuple-element.25), calls=%async_computation.1 | async-start | bytes 4194304 | tf_op jit(solution)/shard_map/all_to_all | solution.py:435
  118.8 1.0 copy-start.4
  119.8 47.4 %copy-start.5 = (f32[32,64,128]{2,1,0:T(8,128)S(1)}, f32[32,64,128]{2,1,0:T(8,128)}, u32[]{:S(2)}) copy-start(f32[32,64,128]{2,1,0:T(8,128)} %copy-done.4) | copy-start | bytes 3145732
  119.8 47.3 %collective-permute-start.16 = (f32[32,64,128]{2,1,0:T(8,128)}, f32[32,64,128]{2,1,0:T(8,128)S(1)}, u32[]{:S(2)}, u32[]{:S(2)}) collective-permute-start(f32[32,64,128]{2,1,0:T(8,128)} %get-tuple-element.31), channel_id=1, source_target_pairs={{0,1},{1,0},{2,3},{3,2},{4,5},{5,4},{6,7},{7,6},{8,9},{9,8},{10,11... | collective-permute-start | bytes 3145736 | tf_op jit(solution)/shard_map/ppermute | solution.py:445
  159.2 9.8 %collective-permute-start.15 = (f32[24,64,128]{2,1,0:T(8,128)S(1)}, f32[24,64,128]{2,1,0:T(8,128)S(1)}, u32[]{:S(2)}, u32[]{:S(2)}) collective-permute-start(f32[24,64,128]{2,1,0:T(8,128)S(1)} %get-tuple-element.27), channel_id=1, source_target_pairs={{0,1},{1,0},{2,3},{3,2},{4,5},{5,4},{6,7},{7,6},{8,9},{9,8},{10,11... | collective-permute-start | bytes 2359304 | tf_op jit(solution)/shard_map/ppermute | solution.py:458
  167.1 1.9 %copy-start = (f32[6144,64]{0,1:T(8,128)S(1)}, f32[6144,64]{0,1:T(8,128)}, u32[]{:S(2)}) copy-start(f32[6144,64]{0,1:T(8,128)} %param.8) | copy-start | bytes 4718596

commit v4 on v3

--- a/solution.py
+++ b/solution.py
@@ -13,7 +13,7 @@
 VMEM = pl.BlockSpec(memory_space=pltpu.VMEM)
 SMEM = pl.BlockSpec(memory_space=pltpu.SMEM)
 HBM = pl.BlockSpec(memory_space=pltpu.HBM)
-GRID = (4, 8, 4)
+TILE = 8
 PARAMS = pltpu.CompilerParams(vmem_limit_bytes=24 << 20)
 
 
@@ -56,18 +56,22 @@
         out_ref[n] = id_ref[:, n * blk : (n + 1) * blk].astype(BF16)
 
 
-def pack_kernel(core_ref, list_ref, keep_ref, recv_ref, out_ref, blocks, chunks, sems):
+def pack_kernel(core_ref, list_ref, keep_ref, recv_ref, count_ref, out_ref, blocks, chunks, weights, sems):
     core = core_ref[0]
     pairs, half_cols, blk = keep_ref.shape
     half = blk // 2
+    weight = count_weight(count_ref[...])
+    weights[...] = jnp.where(core == 0, weight, pltpu.roll(weight, half, 1))
 
     def pair(m, _):
         keep, recv = keep_ref[m].astype(F32), recv_ref[m].astype(F32)
         low = jnp.where(core == 0, keep, recv)
         high = jnp.where(core == 0, recv, keep)
         rows = jnp.concatenate([low, high], axis=0).T.astype(BF16)
-        blocks[2 * m] = rows[:half]
-        blocks[2 * m + 1] = rows[half:]
+        for k in range(2):
+            blocks[2 * m + k, :half] = rows[k * half : (k + 1) * half]
+            weight = jnp.broadcast_to(weights[pl.ds(2 * m + k, 1), :], (TILE, blk))
+            blocks[2 * m + k, half:] = weight.astype(BF16)
         return 0
 
     lax.fori_loop(0, pairs, pair, 0, unroll=4)
@@ -90,28 +94,6 @@
         copies[-1].start()
     for copy in copies:
         copy.wait()
-
-
-def weigh_kernel(core_ref, chip_ref, list_ref, count_ref, out_ref, weights):
-    core = core_ref[0]
-    peers, blk = out_ref.shape
-    weight = count_weight(count_ref[...]).astype(BF16).astype(F32)
-    weights[...] = jnp.where(core == 0, weight, pltpu.roll(weight, blk // 2, 1))
-
-    def row(d, _):
-        out_ref[pl.ds(d, 1), :] = weights[pl.ds(list_ref[combine(chip_ref[0], d, 1)], 1), :]
-        return 0
-
-    lax.fori_loop(0, peers, row, 0, unroll=8)
-
-
-def combine(chip, other, sign):
-    result, shift = 0, 0
-    for n in reversed(GRID):
-        mask = (n - 1) << shift
-        result = result | (((chip & mask) + sign * (other & mask)) & mask)
-        shift += n.bit_length() - 1
-    return result
 
 
 def ident_kernel(core_ref, own_ref, peer_ref, count_ref, idt_ref, id_ref, weight_ref):
@@ -183,7 +165,7 @@
     def step(i, _):
         take(i).wait()
         at = [(i * GROUP + u, slot_ref[i * GROUP + u], ident_ref[i * GROUP + u]) for u in range(GROUP)]
-        scores = [jnp.dot(rows_ref[s], idt_ref[n], preferred_element_type=F32) for _, s, n in at]
+        scores = [jnp.dot(rows_ref[s, :half], idt_ref[n], preferred_element_type=F32) for _, s, n in at]
         resids = []
         for (b, s, n), score in zip(at, scores):
             resid = (weight_ref[pl.ds(n, 1), :] * (score - obs_ref[b].astype(F32))).astype(BF16)
@@ -208,11 +190,9 @@
 
 def ident_grad_kernel(
     core_ref,
-    chip_ref,
     slot_ref,
     ident_ref,
     rows_ref,
-    weight_ref,
     resid_hbm,
     keep_ref,
     send_ref,
@@ -233,8 +213,8 @@
     grad[...] = jnp.zeros_like(grad)
 
     def turn(s, _):
-        rows = rows_ref[s].astype(F32).T
-        weight = weight_ref[pl.ds(combine(chip_ref[0], s, -1), 1), :half]
+        rows = rows_ref[s, :half].astype(F32).T
+        weight = rows_ref[s, half:].astype(F32)[:1, :half]
         turned[s] = (rows * weight).astype(BF16)
         return 0
 
@@ -346,33 +326,9 @@
     return pltpu.with_memory_space_constraint(x, pltpu.HBM)
 
 
-def by_offsets(rows):
-    width = rows.shape[1]
-    chips = GRID[0] * GRID[1] * GRID[2]
-    rows = rows.reshape(*GRID, width)
-    for axis in (0, 2, 1):
-        extent = GRID[axis]
-        stride = 1
-        for n in GRID[axis + 1 :]:
-            stride *= n
-        parts = []
-        for off in range(extent):
-            part = lax.index_in_dim(rows, off, axis, keepdims=False)
-            if off:
-                pairs = []
-                for g in range(chips):
-                    at = (g // stride) % extent
-                    pairs.append((g, g + ((at + off) % extent - at) * stride))
-                part = lax.ppermute(part, "gx", pairs)
-            parts.append(part)
-        rows = jnp.stack(parts, axis)
-    return rows.reshape(chips, width)
-
-
 def body(records, idents, rec_count, id_count, observed, send_list, slot_of_block, id_of_block):
     peers = lax.axis_size("gx")
     core = lax.axis_index("gy").astype(jnp.int32).reshape(1)
-    chip = lax.axis_index("gx").astype(jnp.int32).reshape(1)
     blocks, blk = observed.shape[0], observed.shape[1]
     half_cols = records.shape[1]
     rank = 2 * half_cols
@@ -387,24 +343,20 @@
 
     half_shape = (pairs, half_cols, blk)
     chunk_shape = (peers, half, rank)
+    sent_shape = (peers, half + TILE, rank)
     keep, send = call(
         split_kernel, [(half_shape, BF16)] * 2, [SMEM, HBM], [(rec_t.shape, F32)], [4], name="split"
     )(core, in_hbm(rec_t))
     recv = swap(send)
     (chunks,) = call(
         pack_kernel,
-        [(chunk_shape, BF16, True)],
-        [SMEM, SMEM, VMEM, VMEM],
-        [((recs, half, rank), BF16), (chunk_shape, BF16)],
+        [(sent_shape, BF16, True)],
+        [SMEM, SMEM, VMEM, VMEM, VMEM],
+        [((recs, half + TILE, rank), BF16), (sent_shape, BF16), ((recs, blk), F32)],
         [4],
         name="pack",
-    )(core, in_hbm(sends), keep, recv)
-    late_count, chunks = lax.optimization_barrier((rec_count, chunks))
+    )(core, in_hbm(sends), keep, recv, in_hbm(rec_count))
     arrived = exchange(chunks)
-    (weights,) = call(
-        weigh_kernel, [((peers, blk), F32)], [SMEM, SMEM, SMEM, VMEM], [((recs, blk), F32)], name="weigh"
-    )(core, chip, sends, late_count)
-    arrived_weight = by_offsets(weights)
 
     (id_half,) = call(cast_kernel, [((ids, half_cols, blk), BF16)], [VMEM], name="cast")(id_t)
     id_peer = swap(id_half)
@@ -414,7 +366,6 @@
         [SMEM, VMEM, VMEM, VMEM],
         name="ident",
     )(core, id_half, id_peer, id_count)
-    arrived_weight, id_weight = lax.optimization_barrier((arrived_weight, id_weight))
     resid_shape = (blocks, half, blk)
     groups = blocks // GROUP
     resid, slot_grad = call(
@@ -437,11 +388,11 @@
     id_keep, id_send = call(
         ident_grad_kernel,
         [((ids, half_cols, blk), F32)] * 2,
-        [SMEM] * 4 + [VMEM] * 2 + [HBM],
+        [SMEM] * 3 + [VMEM, HBM],
         [((ids, rank, blk), F32), ((peers, rank, half), BF16), (resid_shape, BF16)],
         [groups],
         name="ident_grad",
-    )(core, chip, slot_of_block, id_of_block, arrived, arrived_weight, in_hbm(resid))
+    )(core, slot_of_block, id_of_block, arrived, in_hbm(resid))
     id_recv = swap(id_send)
     (new_id_t,) = call(ident_update_kernel, [(id_t.shape, F32)], [VMEM] * 3, name="ident_update")(
         id_t, id_keep, id_recv

time: 171 us -> 158 us (0.924)
  starting transfers between devices: 73.3 us -> 34.1 us
  waiting for transfers between devices: 64.2 us -> 91.6 us
    all_to_all x1, waiting for transfers between devices: 0.01 us -> 48.8 us  [body(): arrived = exchange(chunks)]
    ppermute x13 -> x0, waiting for transfers between devices: 30.7 us -> none  [by_offsets(): part = lax.ppermute(part, 'gx', pairs)]
    ppermute x13 -> x0, starting transfers between devices: 25.4 us -> none  [by_offsets(): part = lax.ppermute(part, 'gx', pairs)]
    all_to_all x1, waiting for transfers between devices: 31.5 us -> 39.2 us  [body(): returned = exchange(slot_grad)]
    ppermute x1, starting transfers between devices: 4.83 us -> 1.02 us  [body(): id_recv = swap(id_send)]
    ppermute x1, starting transfers between devices: 7.9 us -> 4.24 us  [body(): rec_recv = swap(rec_send)]
    ppermute x1, starting transfers between devices: 4.03 us -> 0.74 us  [body(): id_peer = swap(id_half)]
    all_to_all x1, starting transfers between devices: 13.9 us -> 10.9 us  [body(): returned = exchange(slot_grad)]
  transfers between devices with their start and end apart: 19 -> 6, of which waited for: 9 -> 5; matrix products, arithmetic and copies ran while one was open for 0% -> 0% of each run, Pallas kernels for 9% -> 9%
where the time goes in v4:
time: 158 us; the launch traced here: 157 us
  waiting for transfers between devices  91.6 us (58%)
  starting transfers between devices  34.1 us (22%)
  Pallas kernels  27.9 us (18%)
  local copies, waits for them, and re-layouts  2.95 us (2%)
    all_to_all x1, waiting for transfers between devices, body(): arrived = exchange(chunks)  48.8 us
    all_to_all x1, waiting for transfers between devices, body(): returned = exchange(slot_grad)  39.2 us
    all_to_all x1, starting transfers between devices, body(): arrived = exchange(chunks)  13.9 us
    all_to_all x1, starting transfers between devices, body(): returned = exchange(slot_grad)  10.9 us
    pallas_call x1, Pallas kernels, body(): call(score_kernel, [(resid_shape, BF16, True), (chunk_shape, BF16, True)]...  8.38 us
    pallas_call x1, Pallas kernels, body(): call(ident_grad_kernel, [((ids, half_cols, blk), F32)] * 2, [SMEM] * 3 +...  7.54 us
    ppermute x1, starting transfers between devices, body(): rec_recv = swap(rec_send)  4.24 us
    ppermute x1, starting transfers between devices, body(): recv = swap(send)  3.33 us
  transfers between devices with their start and end apart: 6, of which 5 were waited for; matrix products, arithmetic and copies ran while one was open for 0% of the time, Pallas kernels for 9%

profile of v4, /device:TPU:1, one launch (start us, length us, event | category | flops | bytes accessed | tf_op | source)
XLA Modules:
  0.0 157.4 jit_solution(2882430801714917504)
XLA Ops:
  0.6 1.5 split.1
  2.2 3.3 %collective-permute-start = (bf16[24,64,128]{2,1,0:T(8,128)(2,1)S(1)}, bf16[24,64,128]{2,1,0:T(8,128)(2,1)S(1)}, u32[]{:S(2)}, u32[]{:S(2)}) collective-permute-start(bf16[24,64,128]{2,1,0:T(8,128)(2,1)S(1)} %get-tuple-element.14), channel_id=1, source_target_pairs={{0,1},{1,0},{2,3},{3,2},{4,5},{5,4},{6,7},{7,6},{8,9},{9,8},{10,11... | collective-permute-start | bytes 1179656 | tf_op jit(solution)/shard_map/ppermute | solution.py:350
  5.5 1.3 collective-permute-done.recv_ref
  6.9 3.0 %pack.1 = bf16[128,72,128]{2,1,0:T(8,128)(2,1)} custom-call(s32[1]{0:T(128)} %bitcast.core_ref, s32[128]{0:T(128)} %bitcast.15, bf16[24,64,128]{2,1,0:T(8,128)(2,1)S(1)} %get-tuple-element.13.keep_ref, bf16[24,64,128]{2,1,0:T(8,128)(2,1)S(1)} %collective-permute-done.recv_ref, s32[48,128]{1,0:T(8,128)} %bitcast.12), custom_call_target="tpu_custom_call" | custom-call | tf_op jit(solution)/shard_map/pack/pallas_call | solution.py:351
  9.9 0.0 copy-start.1
  9.9 0.0 copy-start.7
  9.9 13.9 %all-to-all-start = ((bf16[128,72,128]{2,1,0:T(8,128)(2,1)}), bf16[128,72,128]{2,1,0:T(8,128)(2,1)S(1)}, u32[]{:S(2)}, u32[]{:S(2)}) async-start(bf16[128,72,128]{2,1,0:T(8,128)(2,1)} %pack.1), calls=%async_computation | async-start | bytes 4718592 | tf_op jit(solution)/shard_map/all_to_all | solution.py:359
  23.8 0.0 copy-start.8
  23.8 0.0 copy-start.9
  23.9 0.0 copy-done.1
  23.9 0.1 cast.1.own_ref
  23.9 0.7 collective-permute-start.1
  24.7 1.5 collective-permute-done.1.peer_ref
  26.2 0.0 copy-done.7
  26.2 1.7 %ident.1 = (bf16[32,128,128]{2,1,0:T(8,128)(2,1)S(1)}, bf16[32,128,128]{2,1,0:T(8,128)(2,1)S(1)}, f32[32,128]{1,0:T(8,128)S(1)}) custom-call(s32[1]{0:T(128)} %bitcast.core_ref, bf16[32,64,128]{2,1,0:T(8,128)(2,1)S(1)} %cast.1.own_ref, bf16[32,64,128]{2,1,0:T(8,128)(2,1)S(1)} %collective-permute-done.1.peer_ref, s32[32,128]{1,0:T(8,128)S(1)} %bitcast.14), custom_call_target="tpu_custom_call" | custom-call | tf_op jit(solution)/shard_map/ident/pallas_call | solution.py:363
  27.9 0.0 copy-start.2
  27.9 1.0 copy-done.2
  28.9 0.0 copy-start.3
  28.9 1.0 copy-done.3
  29.9 48.8 %all-to-all-done.rows_ref = bf16[128,72,128]{2,1,0:T(8,128)(2,1)S(1)} async-done(((bf16[128,72,128]{2,1,0:T(8,128)(2,1)}), bf16[128,72,128]{2,1,0:T(8,128)(2,1)S(1)}, u32[]{:S(2)}, u32[]{:S(2)}) %all-to-all-start) | async-done | bytes 2359328 | tf_op jit(solution)/shard_map/all_to_all | solution.py:359
  78.7 0.0 copy-done.8
  78.7 0.0 copy-done.9
  78.7 8.4 %score.1 = (bf16[192,64,128]{2,1,0:T(8,128)(2,1)}, bf16[128,64,128]{2,1,0:T(8,128)(2,1)}) custom-call(s32[1]{0:T(128)} %bitcast.core_ref, s32[192]{0:T(256)S(1)} %copy-done.8, s32[192]{0:T(256)S(1)} %copy-done.9, bf16[128,72,128]{2,1,0:T(8,128)(2,1)S(1)} %all-to-all-done.rows_ref, f32[32,128]{1,0:T(8,128)S(1)} %get-tuple-element.15.weight_ref, ...), custom_call_target="tpu_custom_call" | custom-call | tf_op jit(solution)/shard_map/score/pallas_call | solution.py:371
  87.1 10.9 %all-to-all-start.1 = ((bf16[128,64,128]{2,1,0:T(8,128)(2,1)}), bf16[128,64,128]{2,1,0:T(8,128)(2,1)}, u32[]{:S(2)}, u32[]{:S(2)}) async-start(bf16[128,64,128]{2,1,0:T(8,128)(2,1)} %get-tuple-element.18), calls=%async_computation.1 | async-start | bytes 4194304 | tf_op jit(solution)/shard_map/all_to_all | solution.py:386
  97.9 0.0 copy-start.6
  98.0 0.0 copy-start.10
  98.0 7.5 %ident_grad.1 = (f32[32,64,128]{2,1,0:T(8,128)S(1)}, f32[32,64,128]{2,1,0:T(8,128)}) custom-call(s32[1]{0:T(128)} %bitcast.core_ref, s32[192]{0:T(256)S(1)} %copy-done.8, s32[192]{0:T(256)S(1)} %copy-done.9, bf16[128,72,128]{2,1,0:T(8,128)(2,1)S(1)} %all-to-all-done.rows_ref, bf16[192,64,128]{2,1,0:T(8,128)(2,1)} %get-tuple-element.21.resid_hbm), custom_call_target="tpu_custom_call" | custom-call | tf_op jit(solution)/shard_map/ident_grad/pallas_call | solution.py:388
  105.5 0.0 copy-start.4
  105.5 1.0 copy-done.4
  106.5 0.0 copy-start.5
  106.5 1.0 collective-permute-start.3
  107.5 39.2 %all-to-all-done.1.back_hbm = bf16[128,64,128]{2,1,0:T(8,128)(2,1)} async-done(((bf16[128,64,128]{2,1,0:T(8,128)(2,1)}), bf16[128,64,128]{2,1,0:T(8,128)(2,1)}, u32[]{:S(2)}, u32[]{:S(2)}) %all-to-all-start.1) | async-done | bytes 2097184 | tf_op jit(solution)/shard_map/all_to_all | solution.py:386
  146.7 0.0 copy-done.6
  146.7 0.0 copy-done.10
  146.7 3.2 %collect.1 = (f32[24,64,128]{2,1,0:T(8,128)S(1)}, f32[24,64,128]{2,1,0:T(8,128)S(1)}) custom-call(s32[1]{0:T(128)} %bitcast.core_ref, s32[128]{0:T(128)S(1)} %bitcast.16, bf16[128,64,128]{2,1,0:T(8,128)(2,1)} %all-to-all-done.1.back_hbm, s32[48,128]{1,0:T(8,128)S(1)} %bitcast.13), custom_call_target="tpu_custom_call" | custom-call | tf_op jit(solution)/shard_map/collect/pallas_call | solution.py:401
  149.9 0.0 copy-start
  149.9 4.2 %collective-permute-start.2 = (f32[24,64,128]{2,1,0:T(8,128)S(1)}, f32[24,64,128]{2,1,0:T(8,128)S(1)}, u32[]{:S(2)}, u32[]{:S(2)}) collective-permute-start(f32[24,64,128]{2,1,0:T(8,128)S(1)} %get-tuple-element.20), channel_id=1, source_target_pairs={{0,1},{1,0},{2,3},{3,2},{4,5},{5,4},{6,7},{7,6},{8,9},{9,8},{10,11... | collective-permute-start | bytes 2359304 | tf_op jit(solution)/shard_map/ppermute | solution.py:409
  154.1 0.0 collective-permute-done.3.peer_ref
  154.1 0.0 copy-done.5
  154.1 1.2 ident_update.1
  155.3 0.7 collective-permute-done.2.recv_ref
  156.0 0.0 copy-done
  156.0 1.3 record_update.1
Async XLA Ops:
  2.2 4.7 %collective-permute-start = (bf16[24,64,128]{2,1,0:T(8,128)(2,1)S(1)}, bf16[24,64,128]{2,1,0:T(8,128)(2,1)S(1)}, u32[]{:S(2)}, u32[]{:S(2)}) collective-permute-start(bf16[24,64,128]{2,1,0:T(8,128)(2,1)S(1)} %get-tuple-element.14), channel_id=1, source_target_pairs={{0,1},{1,0},{2,3},{3,2},{4,5},{5,4},{6,7},{7,6},{8,9},{9,8},{10,11... | collective-permute-start | bytes 1179656 | tf_op jit(solution)/shard_map/ppermute | solution.py:350
  9.9 14.0 %copy-start.1 = (f32[4096,64]{0,1:T(8,128)S(1)}, f32[4096,64]{0,1:T(8,128)}, u32[]{:S(2)}) copy-start(f32[4096,64]{0,1:T(8,128)} %param.9) | copy-start | bytes 3145732
  9.9 16.3 %copy-start.7 = (s32[4096]{0:T(1024)S(1)}, s32[4096]{0:T(1024)}, u32[]{:S(2)}) copy-start(s32[4096]{0:T(1024)} %param.11) | copy-start | bytes 49156
  9.9 68.8 %all-to-all-start = ((bf16[128,72,128]{2,1,0:T(8,128)(2,1)}), bf16[128,72,128]{2,1,0:T(8,128)(2,1)S(1)}, u32[]{:S(2)}, u32[]{:S(2)}) async-start(bf16[128,72,128]{2,1,0:T(8,128)(2,1)} %pack.1), calls=%async_computation | async-start | bytes 4718592 | tf_op jit(solution)/shard_map/all_to_all | solution.py:359
  23.8 54.8 %copy-start.8 = (s32[192]{0:T(256)S(1)}, s32[192]{0:T(256)}, u32[]{:S(2)}) copy-start(s32[192]{0:T(256)} %slot_ref.3) | copy-start | bytes 2308
  23.8 54.8 %copy-start.9 = (s32[192]{0:T(256)S(1)}, s32[192]{0:T(256)}, u32[]{:S(2)}) copy-start(s32[192]{0:T(256)} %ident_ref.3) | copy-start | bytes 2308
  23.9 2.3 %collective-permute-start.1 = (bf16[32,64,128]{2,1,0:T(8,128)(2,1)S(1)}, bf16[32,64,128]{2,1,0:T(8,128)(2,1)S(1)}, u32[]{:S(2)}, u32[]{:S(2)}) collective-permute-start(bf16[32,64,128]{2,1,0:T(8,128)(2,1)S(1)} %cast.1.own_ref), channel_id=1, source_target_pairs={{0,1},{1,0},{2,3},{3,2},{4,5},{5,4},{6,7},{7,6},{8,9},{9,8},{10,11... | collective-permute-start | bytes 1572872 | tf_op jit(solution)/shard_map/ppermute | solution.py:362
  27.9 1.0 copy-start.2
  28.9 1.0 copy-start.3
  87.1 59.6 %all-to-all-start.1 = ((bf16[128,64,128]{2,1,0:T(8,128)(2,1)}), bf16[128,64,128]{2,1,0:T(8,128)(2,1)}, u32[]{:S(2)}, u32[]{:S(2)}) async-start(bf16[128,64,128]{2,1,0:T(8,128)(2,1)} %get-tuple-element.18), calls=%async_computation.1 | async-start | bytes 4194304 | tf_op jit(solution)/shard_map/all_to_all | solution.py:386
  97.9 48.8 %copy-start.6 = (s32[6144]{0:T(1024)S(1)}, s32[6144]{0:T(1024)}, u32[]{:S(2)}) copy-start(s32[6144]{0:T(1024)} %param.10) | copy-start | bytes 73732
  98.0 48.8 %copy-start.10 = (s32[128,1]{0,1:T(1,128)S(1)}, s32[128,1]{0,1:T(1,128)}, u32[]{:S(2)}) copy-start(s32[128,1]{0,1:T(1,128)} %param.13) | copy-start | bytes 1540
  105.5 1.0 copy-start.4
  106.5 47.6 %copy-start.5 = (f32[32,64,128]{2,1,0:T(8,128)S(1)}, f32[32,64,128]{2,1,0:T(8,128)}, u32[]{:S(2)}) copy-start(f32[32,64,128]{2,1,0:T(8,128)} %copy-done.4) | copy-start | bytes 3145732
  106.5 47.6 %collective-permute-start.3 = (f32[32,64,128]{2,1,0:T(8,128)}, f32[32,64,128]{2,1,0:T(8,128)S(1)}, u32[]{:S(2)}, u32[]{:S(2)}) collective-permute-start(f32[32,64,128]{2,1,0:T(8,128)} %get-tuple-element.23), channel_id=1, source_target_pairs={{0,1},{1,0},{2,3},{3,2},{4,5},{5,4},{6,7},{7,6},{8,9},{9,8},{10,11... | collective-permute-start | bytes 3145736 | tf_op jit(solution)/shard_map/ppermute | solution.py:396
  149.9 6.2 %copy-start = (f32[6144,64]{0,1:T(8,128)S(1)}, f32[6144,64]{0,1:T(8,128)}, u32[]{:S(2)}) copy-start(f32[6144,64]{0,1:T(8,128)} %param.8) | copy-start | bytes 4718596
  149.9 6.1 %collective-permute-start.2 = (f32[24,64,128]{2,1,0:T(8,128)S(1)}, f32[24,64,128]{2,1,0:T(8,128)S(1)}, u32[]{:S(2)}, u32[]{:S(2)}) collective-permute-start(f32[24,64,128]{2,1,0:T(8,128)S(1)} %get-tuple-element.20), channel_id=1, source_target_pairs={{0,1},{1,0},{2,3},{3,2},{4,5},{5,4},{6,7},{7,6},{8,9},{9,8},{10,11... | collective-permute-start | bytes 2359304 | tf_op jit(solution)/shard_map/ppermute | solution.py:409

commit v5 on v4

--- a/solution.py
+++ b/solution.py
@@ -112,6 +112,7 @@
     weight_ref[...] = count_weight(count_ref[...])
 
 
+SCORE_GROUP = 96
 GROUP = 48
 
 
@@ -138,7 +139,7 @@
     out_sems,
 ):
     blocks, half, _ = obs_ref.shape
-    groups = blocks // GROUP
+    groups = blocks // SCORE_GROUP
     rows_at = pl.ds(pl.multiple_of(core_ref[0] * half, half), half)
     tables = [
         pltpu.make_async_copy(idt_hbm, idt_ref, sems.at[0]),
@@ -146,11 +147,11 @@
     ]
 
     def take(i):
-        at = pl.ds(i * GROUP, GROUP)
+        at = pl.ds(i * SCORE_GROUP, SCORE_GROUP)
         return pltpu.make_async_copy(obs_hbm.at[at, rows_at, :], obs_ref.at[at], in_sems.at[i])
 
     def give(i):
-        at = pl.ds(i * GROUP, GROUP)
+        at = pl.ds(i * SCORE_GROUP, SCORE_GROUP)
         return pltpu.make_async_copy(resid_ref.at[at], resid_hbm.at[at], resid_sems.at[i])
 
     tables[0].start()
@@ -164,7 +165,7 @@
 
     def step(i, _):
         take(i).wait()
-        at = [(i * GROUP + u, slot_ref[i * GROUP + u], ident_ref[i * GROUP + u]) for u in range(GROUP)]
+        at = [(i * SCORE_GROUP + u, slot_ref[i * SCORE_GROUP + u], ident_ref[i * SCORE_GROUP + u]) for u in range(SCORE_GROUP)]
         scores = [jnp.dot(rows_ref[s, :half], idt_ref[n], preferred_element_type=F32) for _, s, n in at]
         resids = []
         for (b, s, n), score in zip(at, scores):
@@ -276,7 +277,7 @@
         both = both * row
         first, last = both[:half_cols], both[half_cols:]
         keep_ref[m] = jnp.where(core == 0, first, last)
-        send_ref[m] = jnp.where(core == 0, last, first)
+        send_ref[m] = jnp.where(core == 0, last, first).astype(BF16)
         return 0
 
     lax.fori_loop(0, pairs, pair, 0, unroll=4)
@@ -290,7 +291,7 @@
     width = out_ref.shape[1] // parts
     copies = []
     for m in range(pairs):
-        keep, recv = keep_ref[m], recv_ref[m]
+        keep, recv = keep_ref[m], recv_ref[m].astype(F32)
         half0 = jnp.where(core == 0, keep, recv)
         half1 = jnp.where(core == 0, recv, keep)
         grads = (
@@ -368,6 +369,7 @@
     )(core, id_half, id_peer, id_count)
     resid_shape = (blocks, half, blk)
     groups = blocks // GROUP
+    score_groups = blocks // SCORE_GROUP
     resid, slot_grad = call(
         score_kernel,
         [(resid_shape, BF16, True), (chunk_shape, BF16, True)],
@@ -380,7 +382,7 @@
             (chunk_shape, F32),
             (chunk_shape, BF16),
         ],
-        [2, groups, groups, 4],
+        [2, score_groups, score_groups, 4],
         name="score",
     )(core, slot_of_block, id_of_block, arrived, id_weight, in_hbm(idt), in_hbm(id_rows), in_hbm(observed))
     returned = exchange(slot_grad)
@@ -400,7 +402,7 @@
 
     rec_keep, rec_send = call(
         collect_kernel,
-        [(half_shape, F32), (half_shape, F32)],
+        [(half_shape, F32), (half_shape, BF16)],
         [SMEM, SMEM, HBM, VMEM],
         [((recs, half, rank), F32), ((recs, blk), F32), (chunk_shape, BF16)],
         [8],

time: 158 us -> 157 us (level)
  no operation moved by 1% of the time
where the time goes in v5:
time: 157 us
  waiting for transfers between devices  91.1 us (58%)
  starting transfers between devices  34.1 us (22%)
  Pallas kernels  27.6 us (18%)
  local copies, waits for them, and re-layouts  2.95 us (2%)
    all_to_all x1, waiting for transfers between devices, body(): arrived = exchange(chunks)  48.8 us
    all_to_all x1, waiting for transfers between devices, body(): returned = exchange(slot_grad)  39.2 us
    all_to_all x1, starting transfers between devices, body(): arrived = exchange(chunks)  13.9 us
    all_to_all x1, starting transfers between devices, body(): returned = exchange(slot_grad)  10.9 us
    pallas_call x1, Pallas kernels, body(): call(score_kernel, [(resid_shape, BF16, True), (chunk_shape, BF16, True)]...  8.07 us
    pallas_call x1, Pallas kernels, body(): call(ident_grad_kernel, [((ids, half_cols, blk), F32)] * 2, [SMEM] * 3 +...  7.53 us
    ppermute x1, starting transfers between devices, body(): rec_recv = swap(rec_send)  4.24 us
    ppermute x1, starting transfers between devices, body(): recv = swap(send)  3.33 us
  transfers between devices with their start and end apart: 6, of which 5 were waited for; matrix products, arithmetic and copies ran while one was open for 0% of the time, Pallas kernels for 9%

profile of v5, /device:TPU:1, one launch (start us, length us, event | category | flops | bytes accessed | tf_op | source)
XLA Modules:
  0.0 156.5 jit_solution(7059806427182090473)
XLA Ops:
  0.6 1.5 split.1
  2.2 3.3 %collective-permute-start = (bf16[24,64,128]{2,1,0:T(8,128)(2,1)S(1)}, bf16[24,64,128]{2,1,0:T(8,128)(2,1)S(1)}, u32[]{:S(2)}, u32[]{:S(2)}) collective-permute-start(bf16[24,64,128]{2,1,0:T(8,128)(2,1)S(1)} %get-tuple-element.14), channel_id=1, source_target_pairs={{0,1},{1,0},{2,3},{3,2},{4,5},{5,4},{6,7},{7,6},{8,9},{9,8},{10,11... | collective-permute-start | bytes 1179656 | tf_op jit(solution)/shard_map/ppermute | solution.py:351
  5.5 1.3 collective-permute-done.recv_ref
  6.9 3.0 %pack.1 = bf16[128,72,128]{2,1,0:T(8,128)(2,1)} custom-call(s32[1]{0:T(128)} %bitcast.core_ref, s32[128]{0:T(128)} %bitcast.15, bf16[24,64,128]{2,1,0:T(8,128)(2,1)S(1)} %get-tuple-element.13.keep_ref, bf16[24,64,128]{2,1,0:T(8,128)(2,1)S(1)} %collective-permute-done.recv_ref, s32[48,128]{1,0:T(8,128)} %bitcast.12), custom_call_target="tpu_custom_call" | custom-call | tf_op jit(solution)/shard_map/pack/pallas_call | solution.py:352
  9.9 0.0 copy-start.1
  9.9 0.0 copy-start.7
  9.9 13.9 %all-to-all-start = ((bf16[128,72,128]{2,1,0:T(8,128)(2,1)}), bf16[128,72,128]{2,1,0:T(8,128)(2,1)S(1)}, u32[]{:S(2)}, u32[]{:S(2)}) async-start(bf16[128,72,128]{2,1,0:T(8,128)(2,1)} %pack.1), calls=%async_computation | async-start | bytes 4718592 | tf_op jit(solution)/shard_map/all_to_all | solution.py:360
  23.8 0.0 copy-start.8
  23.8 0.0 copy-start.9
  23.9 0.0 copy-done.1
  23.9 0.1 cast.1.own_ref
  23.9 0.7 collective-permute-start.1
  24.7 1.5 collective-permute-done.1.peer_ref
  26.2 0.0 copy-done.7
  26.2 1.7 %ident.1 = (bf16[32,128,128]{2,1,0:T(8,128)(2,1)S(1)}, bf16[32,128,128]{2,1,0:T(8,128)(2,1)S(1)}, f32[32,128]{1,0:T(8,128)S(1)}) custom-call(s32[1]{0:T(128)} %bitcast.core_ref, bf16[32,64,128]{2,1,0:T(8,128)(2,1)S(1)} %cast.1.own_ref, bf16[32,64,128]{2,1,0:T(8,128)(2,1)S(1)} %collective-permute-done.1.peer_ref, s32[32,128]{1,0:T(8,128)S(1)} %bitcast.14), custom_call_target="tpu_custom_call" | custom-call | tf_op jit(solution)/shard_map/ident/pallas_call | solution.py:364
  27.9 0.0 copy-start.2
  27.9 1.0 copy-done.2
  28.9 0.0 copy-start.3
  28.9 1.0 copy-done.3
  29.9 48.8 %all-to-all-done.rows_ref = bf16[128,72,128]{2,1,0:T(8,128)(2,1)S(1)} async-done(((bf16[128,72,128]{2,1,0:T(8,128)(2,1)}), bf16[128,72,128]{2,1,0:T(8,128)(2,1)S(1)}, u32[]{:S(2)}, u32[]{:S(2)}) %all-to-all-start) | async-done | bytes 2359328 | tf_op jit(solution)/shard_map/all_to_all | solution.py:360
  78.7 0.0 copy-done.8
  78.7 0.0 copy-done.9
  78.7 8.1 %score.1 = (bf16[192,64,128]{2,1,0:T(8,128)(2,1)}, bf16[128,64,128]{2,1,0:T(8,128)(2,1)}) custom-call(s32[1]{0:T(128)} %bitcast.core_ref, s32[192]{0:T(256)S(1)} %copy-done.8, s32[192]{0:T(256)S(1)} %copy-done.9, bf16[128,72,128]{2,1,0:T(8,128)(2,1)S(1)} %all-to-all-done.rows_ref, f32[32,128]{1,0:T(8,128)S(1)} %get-tuple-element.15.weight_ref, ...), custom_call_target="tpu_custom_call" | custom-call | tf_op jit(solution)/shard_map/score/pallas_call | solution.py:373
  86.8 10.9 %all-to-all-start.1 = ((bf16[128,64,128]{2,1,0:T(8,128)(2,1)}), bf16[128,64,128]{2,1,0:T(8,128)(2,1)}, u32[]{:S(2)}, u32[]{:S(2)}) async-start(bf16[128,64,128]{2,1,0:T(8,128)(2,1)} %get-tuple-element.18), calls=%async_computation.1 | async-start | bytes 4194304 | tf_op jit(solution)/shard_map/all_to_all | solution.py:388
  97.6 0.0 copy-start.6
  97.6 0.0 copy-start.10
  97.7 7.5 %ident_grad.1 = (f32[32,64,128]{2,1,0:T(8,128)S(1)}, f32[32,64,128]{2,1,0:T(8,128)}) custom-call(s32[1]{0:T(128)} %bitcast.core_ref, s32[192]{0:T(256)S(1)} %copy-done.8, s32[192]{0:T(256)S(1)} %copy-done.9, bf16[128,72,128]{2,1,0:T(8,128)(2,1)S(1)} %all-to-all-done.rows_ref, bf16[192,64,128]{2,1,0:T(8,128)(2,1)} %get-tuple-element.21.resid_hbm), custom_call_target="tpu_custom_call" | custom-call | tf_op jit(solution)/shard_map/ident_grad/pallas_call | solution.py:390
  105.2 0.0 copy-start.4
  105.2 1.0 copy-done.4
  106.2 0.0 copy-start.5
  106.2 1.0 collective-permute-start.3
  107.2 39.2 %all-to-all-done.1.back_hbm = bf16[128,64,128]{2,1,0:T(8,128)(2,1)} async-done(((bf16[128,64,128]{2,1,0:T(8,128)(2,1)}), bf16[128,64,128]{2,1,0:T(8,128)(2,1)}, u32[]{:S(2)}, u32[]{:S(2)}) %all-to-all-start.1) | async-done | bytes 2097184 | tf_op jit(solution)/shard_map/all_to_all | solution.py:388
  146.4 0.0 copy-done.6
  146.4 0.0 copy-done.10
  146.4 3.2 %collect.1 = (f32[24,64,128]{2,1,0:T(8,128)S(1)}, bf16[24,64,128]{2,1,0:T(8,128)(2,1)S(1)}) custom-call(s32[1]{0:T(128)} %bitcast.core_ref, s32[128]{0:T(128)S(1)} %bitcast.16, bf16[128,64,128]{2,1,0:T(8,128)(2,1)} %all-to-all-done.1.back_hbm, s32[48,128]{1,0:T(8,128)S(1)} %bitcast.13), custom_call_target="tpu_custom_call" | custom-call | tf_op jit(solution)/shard_map/collect/pallas_call | solution.py:403
  149.6 0.0 copy-start
  149.6 4.2 %collective-permute-start.2 = (bf16[24,64,128]{2,1,0:T(8,128)(2,1)S(1)}, bf16[24,64,128]{2,1,0:T(8,128)(2,1)S(1)}, u32[]{:S(2)}, u32[]{:S(2)}) collective-permute-start(bf16[24,64,128]{2,1,0:T(8,128)(2,1)S(1)} %get-tuple-element.20), channel_id=1, source_target_pairs={{0,1},{1,0},{2,3},{3,2},{4,5},{5,4},{6,7},{7,6},{8,9},{9,8},{10,11... | collective-permute-start | bytes 1179656 | tf_op jit(solution)/shard_map/ppermute | solution.py:411
  153.8 0.0 collective-permute-done.3.peer_ref
  153.8 0.0 copy-done.5
  153.8 1.2 ident_update.1
  155.0 0.2 collective-permute-done.2.recv_ref
  155.2 0.0 copy-done
  155.2 1.3 record_update.1
Async XLA Ops:
  2.2 4.7 %collective-permute-start = (bf16[24,64,128]{2,1,0:T(8,128)(2,1)S(1)}, bf16[24,64,128]{2,1,0:T(8,128)(2,1)S(1)}, u32[]{:S(2)}, u32[]{:S(2)}) collective-permute-start(bf16[24,64,128]{2,1,0:T(8,128)(2,1)S(1)} %get-tuple-element.14), channel_id=1, source_target_pairs={{0,1},{1,0},{2,3},{3,2},{4,5},{5,4},{6,7},{7,6},{8,9},{9,8},{10,11... | collective-permute-start | bytes 1179656 | tf_op jit(solution)/shard_map/ppermute | solution.py:351
  9.9 14.0 %copy-start.1 = (f32[4096,64]{0,1:T(8,128)S(1)}, f32[4096,64]{0,1:T(8,128)}, u32[]{:S(2)}) copy-start(f32[4096,64]{0,1:T(8,128)} %param.9) | copy-start | bytes 3145732
  9.9 16.3 %copy-start.7 = (s32[4096]{0:T(1024)S(1)}, s32[4096]{0:T(1024)}, u32[]{:S(2)}) copy-start(s32[4096]{0:T(1024)} %param.11) | copy-start | bytes 49156
  9.9 68.8 %all-to-all-start = ((bf16[128,72,128]{2,1,0:T(8,128)(2,1)}), bf16[128,72,128]{2,1,0:T(8,128)(2,1)S(1)}, u32[]{:S(2)}, u32[]{:S(2)}) async-start(bf16[128,72,128]{2,1,0:T(8,128)(2,1)} %pack.1), calls=%async_computation | async-start | bytes 4718592 | tf_op jit(solution)/shard_map/all_to_all | solution.py:360
  23.8 54.8 %copy-start.8 = (s32[192]{0:T(256)S(1)}, s32[192]{0:T(256)}, u32[]{:S(2)}) copy-start(s32[192]{0:T(256)} %slot_ref.3) | copy-start | bytes 2308
  23.8 54.8 %copy-start.9 = (s32[192]{0:T(256)S(1)}, s32[192]{0:T(256)}, u32[]{:S(2)}) copy-start(s32[192]{0:T(256)} %ident_ref.3) | copy-start | bytes 2308
  23.9 2.3 %collective-permute-start.1 = (bf16[32,64,128]{2,1,0:T(8,128)(2,1)S(1)}, bf16[32,64,128]{2,1,0:T(8,128)(2,1)S(1)}, u32[]{:S(2)}, u32[]{:S(2)}) collective-permute-start(bf16[32,64,128]{2,1,0:T(8,128)(2,1)S(1)} %cast.1.own_ref), channel_id=1, source_target_pairs={{0,1},{1,0},{2,3},{3,2},{4,5},{5,4},{6,7},{7,6},{8,9},{9,8},{10,11... | collective-permute-start | bytes 1572872 | tf_op jit(solution)/shard_map/ppermute | solution.py:363
  27.9 1.0 copy-start.2
  28.9 1.0 copy-start.3
  86.8 59.6 %all-to-all-start.1 = ((bf16[128,64,128]{2,1,0:T(8,128)(2,1)}), bf16[128,64,128]{2,1,0:T(8,128)(2,1)}, u32[]{:S(2)}, u32[]{:S(2)}) async-start(bf16[128,64,128]{2,1,0:T(8,128)(2,1)} %get-tuple-element.18), calls=%async_computation.1 | async-start | bytes 4194304 | tf_op jit(solution)/shard_map/all_to_all | solution.py:388
  97.6 48.8 %copy-start.6 = (s32[6144]{0:T(1024)S(1)}, s32[6144]{0:T(1024)}, u32[]{:S(2)}) copy-start(s32[6144]{0:T(1024)} %param.10) | copy-start | bytes 73732
  97.6 48.8 %copy-start.10 = (s32[128,1]{0,1:T(1,128)S(1)}, s32[128,1]{0,1:T(1,128)}, u32[]{:S(2)}) copy-start(s32[128,1]{0,1:T(1,128)} %param.13) | copy-start | bytes 1540
  105.2 1.0 copy-start.4
  106.2 47.7 %copy-start.5 = (f32[32,64,128]{2,1,0:T(8,128)S(1)}, f32[32,64,128]{2,1,0:T(8,128)}, u32[]{:S(2)}) copy-start(f32[32,64,128]{2,1,0:T(8,128)} %copy-done.4) | copy-start | bytes 3145732
  106.2 47.6 %collective-permute-start.3 = (f32[32,64,128]{2,1,0:T(8,128)}, f32[32,64,128]{2,1,0:T(8,128)S(1)}, u32[]{:S(2)}, u32[]{:S(2)}) collective-permute-start(f32[32,64,128]{2,1,0:T(8,128)} %get-tuple-element.23), channel_id=1, source_target_pairs={{0,1},{1,0},{2,3},{3,2},{4,5},{5,4},{6,7},{7,6},{8,9},{9,8},{10,11... | collective-permute-start | bytes 3145736 | tf_op jit(solution)/shard_map/ppermute | solution.py:398
  149.6 5.6 %copy-start = (f32[6144,64]{0,1:T(8,128)S(1)}, f32[6144,64]{0,1:T(8,128)}, u32[]{:S(2)}) copy-start(f32[6144,64]{0,1:T(8,128)} %param.8) | copy-start | bytes 4718596
  149.6 5.6 %collective-permute-start.2 = (bf16[24,64,128]{2,1,0:T(8,128)(2,1)S(1)}, bf16[24,64,128]{2,1,0:T(8,128)(2,1)S(1)}, u32[]{:S(2)}, u32[]{:S(2)}) collective-permute-start(bf16[24,64,128]{2,1,0:T(8,128)(2,1)S(1)} %get-tuple-element.20), channel_id=1, source_target_pairs={{0,1},{1,0},{2,3},{3,2},{4,5},{5,4},{6,7},{7,6},{8,9},{9,8},{10,11... | collective-permute-start | bytes 1179656 | tf_op jit(solution)/shard_map/ppermute | solution.py:411
